TPU v7x, 32 devices: a whole 2x2x4 slice. The times are simulated.
32 devices in a mesh: dp: 2 (over x), ctx: 4 (over z), tp: 4 (over y, core).
Axes of the slice: x: 2, y: 2, z: 4, core: 2. Of those that a mesh axis runs over, the one named last changes fastest.
Arguments:
- block_input: bfloat16 [4, 4096, 768], P('dp', ('ctx', 'tp')), may hold values from -6 to 6
- lengths: int32 [4], P('dp'), may hold values from 1024 to 4096, as said below
- cotangent: bfloat16 [4, 4096, 768], P('dp', ('ctx', 'tp')), may hold values from -6 to 6
- query_weight: float32 [768, 768], P(('dp', 'ctx'), 'tp'), may hold values from -0.3125 to 0.3125
- query_bias: float32 [768], P('tp'), may hold values from -3 to 3
- key_weight: float32 [768, 768], P(('dp', 'ctx'), 'tp'), may hold values from -0.21875 to 0.21875
- value_weight: float32 [768, 768], P(('dp', 'ctx'), 'tp'), may hold values from -0.21875 to 0.21875
- value_bias: float32 [768], P('tp'), may hold values from -3 to 3
- output_weight: float32 [768, 768], P('tp', ('dp', 'ctx')), may hold values from -0.875 to 0.875
- output_bias: float32 [768], replicated, may hold values from -3 to 3
- first_gain: float32 [768], replicated, may hold values from 0.25 to 1.75
- first_shift: float32 [768], replicated, may hold values from -3 to 3
- inner_weight: float32 [768, 3072], P(('dp', 'ctx'), 'tp'), may hold values from -0.21875 to 0.21875
- inner_bias: float32 [3072], P('tp'), may hold values from -3 to 3
- outer_weight: float32 [3072, 768], P('tp', ('dp', 'ctx')), may hold values from -0.21875 to 0.21875
- closing_offset_vector: float32 [768], replicated, may hold values from -3 to 3
- second_gain: float32 [768], replicated, may hold values from 0.25 to 1.75
- second_shift: float32 [768], replicated, may hold values from -3 to 3
Outputs:
- output: float32 [4, 4096, 768], P('dp', ('ctx', 'tp'))
- input_grad: float32 [4, 4096, 768], P('dp', ('ctx', 'tp'))
- query_weight_grad: float32 [768, 768], P(('dp', 'ctx'), 'tp')
- query_bias_grad: float32 [768], P('tp')
- key_weight_grad: float32 [768, 768], P(('dp', 'ctx'), 'tp')
- value_weight_grad: float32 [768, 768], P(('dp', 'ctx'), 'tp')
- value_bias_grad: float32 [768], P('tp')
- output_weight_grad: float32 [768, 768], P('tp', ('dp', 'ctx'))
- output_bias_grad: float32 [768], replicated
- first_gain_grad: float32 [768], replicated
- first_shift_grad: float32 [768], replicated
- inner_weight_grad: float32 [768, 3072], P(('dp', 'ctx'), 'tp')
- inner_bias_grad: float32 [3072], P('tp')
- outer_weight_grad: float32 [3072, 768], P('tp', ('dp', 'ctx'))
- outer_bias_grad: float32 [768], replicated
- second_gain_grad: float32 [768], replicated
- second_shift_grad: float32 [768], replicated
Inputs may be any that keep to these rules, and one draw needn't show every extreme that they name: `lengths`: valid slots come first in each sequence; some sequence has exactly 4096 valid slots and another exactly 1024.
All inputs are finite; a program needn't handle non-finite values.
Results may differ from a plain program's by a relative error of at most 0.02.
The roundings to bfloat16 on the way count: a program that leaves them out, or rounds other values in their place, can miss the bound.
Values may be sent and summed in bfloat16 or wider, within the bound.
No kernel may reach another device: no remote copies, remote signals or barrier semaphores. Data moves between devices by JAX's collectives and lax.ppermute only.
A program may use at most 192 MiB of HBM per device.

v0:
```python
import functools
import math

import jax
import jax.numpy as jnp
from jax import lax
from jax.experimental import pallas as pl
from jax.experimental.pallas import tpu as pltpu
from jax.sharding import PartitionSpec as P

HD = 64
PAIR = 2 * HD
EPSILON = 1e-12
NEGATIVE = -1e30
LARGEST = 1e30
BF = jnp.bfloat16
F32 = jnp.float32
VMEM_LIMIT = 56 << 20
FEED_ROWS = 256

NN = (((1,), (0,)), ((), ()))
NT = (((1,), (1,)), ((), ()))
TN = (((0,), (0,)), ((), ()))


def dot(a, b, dims):
    return lax.dot_general(a, b, dims, preferred_element_type=F32)


def params():
    return pltpu.CompilerParams(vmem_limit_bytes=VMEM_LIMIT)


def cost(flops, moved, transcendentals=0):
    return pl.CostEstimate(flops=int(flops), bytes_accessed=int(moved), transcendentals=int(transcendentals))


def after(value, *others):
    if not others:
        return value
    return lax.optimization_barrier((value, *others))[0]


def swap(value, axis, bit, start=(), done=()):
    count = lax.axis_size(axis)
    return after(lax.ppermute(after(value, *start), axis, [(i, i ^ bit) for i in range(count)]), *done)


def bits_of(axis):
    count = lax.axis_size(axis)
    return [1 << k for k in range(count.bit_length() - 1)]


def halves(value, upper, dim):
    size = value.shape[dim] // 2
    at = upper.astype(jnp.int32) * size
    mine = lax.dynamic_slice_in_dim(value, at, size, dim)
    return mine, lax.dynamic_slice_in_dim(value, size - at, size, dim)


def ordered(mine, other, upper, dim):
    return jnp.concatenate([jnp.where(upper, other, mine), jnp.where(upper, mine, other)], axis=dim)


def call(kernel, name, outs, *arrays, prefetch=None, scratch=(), flops=0):
    spec = lambda shape: pl.BlockSpec(shape, lambda i, *c: (0,) * len(shape))
    arrays_moved = sum(a.size * a.dtype.itemsize for a in arrays) + sum(4 * math.prod(shape) for shape, _ in outs)
    return pl.pallas_call(
        kernel,
        grid_spec=pltpu.PrefetchScalarGridSpec(
            num_scalar_prefetch=0 if prefetch is None else 1,
            grid=(1,),
            in_specs=[spec(a.shape) for a in arrays],
            out_specs=[spec(shape) for shape, _ in outs],
            scratch_shapes=list(scratch),
        ),
        out_shape=[jax.ShapeDtypeStruct(shape, kind) for shape, kind in outs],
        compiler_params=params(),
        cost_estimate=cost(flops, arrays_moved),
        name=name,
    )(*(() if prefetch is None else (prefetch,)), *arrays)


def fits(rows):
    return rows % 16 == 0


def pack(groups):
    flat = [piece for group in groups for piece in group]
    widths = [sum(w.shape[0] if t else w.shape[1] for w, t in group) for group in groups]
    first, turned = flat[0]
    rows = first.shape[1] if turned else first.shape[0]

    def joined(values):
        values, out = list(values), []
        for group, width in zip(groups, widths):
            out += [values.pop(0) for _ in group]
            if -width % 128:
                out.append(jnp.zeros((rows, -width % 128), F32))
        return jnp.concatenate(out, axis=1).astype(BF)

    if not fits(rows):
        return joined(w.T if t else w for w, t in flat)

    def kernel(*refs):
        refs[-1][...] = joined(r[...].T if t else r[...] for r, (_, t) in zip(refs, flat))

    total = sum(w + -w % 128 for w in widths)
    return call(kernel, "pack", [((rows, total), BF)], *[w for w, _ in flat])[0]


def stack(parts, cuts=None):
    rows, width = parts[0].shape
    ranges = [(0, width)] if cuts is None else [(0, cuts), (cuts, width)]
    if not fits(rows):
        whole = jnp.concatenate(parts, axis=0)
        return [whole[:, start:stop] for start, stop in ranges]

    def kernel(*refs):
        for k, ref in enumerate(refs[: len(parts)]):
            for out, (start, stop) in zip(refs[len(parts) :], ranges):
                out[k * rows : k * rows + rows, :] = ref[:, start:stop]

    return call(kernel, "stack", [((rows * len(parts), stop - start), BF) for start, stop in ranges], *parts)


def over_dp(arrays, done=()):
    found = [arrays]
    for bit in bits_of("dp"):
        found = found + [[swap(a, "dp", bit, (), done) for a in one] for one in found]
    return found


def place(found, widths, joined):
    spots, spot = lax.axis_size("ctx"), lax.axis_index("ctx")
    line, side = lax.axis_index("dp"), lax.axis_index("tp") // 2
    lines = len(found)
    starts = [sum(widths[:k]) for k in range(len(widths))]
    block = found[0][0].shape[0]
    rows = block // spots
    cuts = list(zip(starts, widths))
    shapes = [(block * lines, 2 * sum(widths[m] for m in members)) for members in joined]
    if not fits(rows):
        order = ((jnp.arange(lines)[:, None] ^ line) * spots + (jnp.arange(spots)[None, :] ^ spot)).reshape(-1)
        own, oth = (
            jnp.stack([f[h] for f in found]).reshape(lines * spots, rows, -1)[order].reshape(lines * block, -1)
            for h in range(2)
        )
        low, high = jnp.where(side == 1, oth, own), jnp.where(side == 1, own, oth)
        full = [jnp.concatenate([low[:, t : t + w], high[:, t : t + w]], axis=1) for t, w in cuts]
        return [full[m[0]] if len(m) == 1 else interleaved(full[m[0]], full[m[1]]) for m in joined]

    def kernel(where, *refs):
        outs = refs[2 * lines :]
        upper = where[2] == 1
        for k in range(lines):
            own_ref, oth_ref = refs[2 * k], refs[2 * k + 1]
            for c in range(spots):
                came = pl.ds(pl.multiple_of((where[0] ^ c) * rows, rows), rows)
                to = pl.ds(pl.multiple_of(((where[1] ^ k) * spots + c) * rows, rows), rows)
                own, oth = own_ref[came, :], oth_ref[came, :]
                low, high = jnp.where(upper, oth, own), jnp.where(upper, own, oth)
                full = [jnp.concatenate([low[:, t : t + w], high[:, t : t + w]], axis=1) for t, w in cuts]
                for out, members in zip(outs, joined):
                    if len(members) == 1:
                        out[to, :] = full[members[0]]
                    else:
                        both = []
                        for p in range(0, full[members[0]].shape[1], PAIR):
                            both += [full[m][:, p : p + PAIR] for m in members]
                        out[to, :] = jnp.concatenate(both, axis=1)

    where = jnp.stack([spot, line, side]).astype(jnp.int32)
    flat = [a for one in found for a in one]
    return call(kernel, "place", [(shape, BF) for shape in shapes], *flat, prefetch=where)


def fold_sides(pairs, cuts, kind=F32):
    rows = pairs[0][0].shape[0]
    width = sum(w for low, _ in cuts for _, _, w in low)
    spare = -width % 128
    width += spare
    side = lax.axis_index("tp") // 2

    def both(totals):
        end = [jnp.zeros((totals[0].shape[0], spare), F32)] if spare else []
        low = jnp.concatenate([totals[p][:, t : t + w] for cut, _ in cuts for p, t, w in cut] + end, axis=1)
        high = jnp.concatenate([totals[p][:, t : t + w] for _, cut in cuts for p, t, w in cut] + end, axis=1)
        return low, high

    if not fits(rows):
        low, high = both([a.astype(F32) + b.astype(F32) for a, b in pairs])
        return jnp.where(side == 1, high, low).astype(kind), jnp.where(side == 1, low, high).astype(BF)

    block = rows // 2 if fits(rows // 2) else rows
    steps = rows // block

    def kernel(where, *refs):
        kept, sent = refs[2 * len(pairs) :]
        totals = [refs[2 * k][...].astype(F32) + refs[2 * k + 1][...].astype(F32) for k in range(len(pairs))]
        low, high = both(totals)
        upper = where[0] == 1
        kept[...] = jnp.where(upper, high, low).astype(kind)
        sent[...] = jnp.where(upper, low, high).astype(BF)

    spec = lambda w: pl.BlockSpec((block, w), lambda i, c: (i, 0))
    flat = [a for pair in pairs for a in pair]
    return pl.pallas_call(
        kernel,
        grid_spec=pltpu.PrefetchScalarGridSpec(
            num_scalar_prefetch=1,
            grid=(steps,),
            in_specs=[spec(a.shape[1]) for a in flat],
            out_specs=[spec(width), spec(width)],
        ),
        out_shape=[jax.ShapeDtypeStruct((rows, width), kind), jax.ShapeDtypeStruct((rows, width), BF)],
        compiler_params=params(),
        cost_estimate=cost(0, sum(a.size * a.dtype.itemsize for a in flat) + 6 * rows * width),
        name="fold_sides",
    )(side.astype(jnp.int32).reshape(1), *flat)


def fold_spots(kept, came, vector):
    spots, spot = lax.axis_size("ctx"), lax.axis_index("ctx")
    rows, width = kept.shape[0] // spots, kept.shape[1]
    count = vector.shape[0]
    below_rows = 3 * count + -3 * count % 16
    if not fits(rows):
        total = kept + came.astype(F32)
        cut = lambda k: lax.dynamic_slice_in_dim(total, (spot ^ k) * rows, rows, 0)
        terms = jnp.concatenate([*in_three(vector), jnp.zeros((below_rows - 3 * count, width), BF)], axis=0)
        return [cut(0)] + [jnp.concatenate([cut(k).astype(BF), terms], axis=0) for k in range(1, spots)]

    def kernel(where, kept_ref, came_ref, vector_ref, own, *outs):
        at = pl.ds(pl.multiple_of(where[0] * rows, rows), rows)
        own[...] = kept_ref[at, :] + came_ref[at, :].astype(F32)
        terms = jnp.concatenate(in_three(vector_ref[...]), axis=0)
        terms = jnp.concatenate([terms, jnp.zeros((below_rows - 3 * count, width), BF)], axis=0)
        for k, out in enumerate(outs):
            at = pl.ds(pl.multiple_of((where[0] ^ (k + 1)) * rows, rows), rows)
            out[:rows, :] = (kept_ref[at, :] + came_ref[at, :].astype(F32)).astype(BF)
            out[rows:, :] = terms

    outs = [((rows, width), F32)] + [((rows + below_rows, width), BF)] * (spots - 1)
    return call(kernel, "fold_spots", outs, kept, came, vector, prefetch=spot.astype(jnp.int32).reshape(1))


def add_low(kept, came):
    if not fits(kept.shape[0] // 2):
        return (kept.astype(F32) + came.astype(F32)).astype(BF)

    def kernel(kept_ref, came_ref, out):
        out[...] = (kept_ref[...].astype(F32) + came_ref[...].astype(F32)).astype(BF)

    rows, width = kept.shape
    spec = pl.BlockSpec((rows // 2, width), lambda i: (i, 0))
    return pl.pallas_call(
        kernel,
        grid=(2,),
        in_specs=[spec, spec],
        out_specs=spec,
        out_shape=jax.ShapeDtypeStruct(kept.shape, BF),
        compiler_params=params(),
        cost_estimate=cost(kept.size, 8 * kept.size),
        name="add_low",
    )(kept, came)


def own_rows(where, value, rows):
    mine = pl.ds(pl.multiple_of(where * rows, rows), rows)
    other = pl.ds(pl.multiple_of((1 - where) * rows, rows), rows)
    return value[mine, :], value[other, :]


def assemble(upper, pieces, held):
    local = pieces[0].shape[0]
    for k in range(len(pieces) // 2):
        mine, came = pieces[2 * k][...], pieces[2 * k + 1][...]
        held[2 * k * local : (2 * k + 1) * local, :] = jnp.where(upper, came, mine)
        held[(2 * k + 1) * local : (2 * k + 2) * local, :] = jnp.where(upper, mine, came)


def query_back_kernel(seqs, lines, where, *refs):
    dq_own, dq_came, own, came = (refs[k * seqs : k * seqs + seqs] for k in range(4))
    weight, mine_ref, other_ref, bias_ref = refs[4 * seqs : 4 * seqs + 4]
    weight_refs, total = refs[4 * seqs + 4 : -1], refs[-1]
    upper = where[0] == 1
    half = own[0].shape[0]
    bias = None
    for s in range(seqs):
        low = (dq_own[s][...] + dq_came[s][...].astype(F32)).astype(BF)
        rows = jnp.concatenate(
            [jnp.where(upper, came[s][...], own[s][...]), jnp.where(upper, own[s][...], came[s][...])], axis=0
        )
        part = dot(low, weight[...], (((0,), (1,)), ((), ())))
        to = slice(s * half, s * half + half)
        mine_ref[to, :] = jnp.where(upper, part[half:], part[:half])
        other_ref[to, :] = jnp.where(upper, part[:half], part[half:]).astype(BF)
        grad = dot(rows, low, (((0,), (1,)), ((), ())))
        total[...] = grad if s == 0 else total[...] + grad
        sums = jnp.sum(low.astype(F32), axis=1, keepdims=True)
        bias = sums if bias is None else bias + sums
    bias_ref[...] = bias
    if lines == 2:
        kept, sent = own_rows(where[1], total, total.shape[0] // 2)
        weight_refs[0][...] = kept
        weight_refs[1][...] = sent.astype(BF)
    else:
        weight_refs[0][...] = total[...]


def query_back(where, dq_own, dq_came, own, came, weight):
    seqs, lines = len(dq_own), lax.axis_size("dp")
    local, width = own[0].shape
    own_width = weight.shape[1]
    outs = [((seqs * local, width), F32), ((seqs * local, width), BF), ((own_width, 1), F32)]
    if lines == 2:
        outs += [((width // 2, own_width), F32), ((width // 2, own_width), BF)]
    else:
        outs += [((width, own_width), F32)]
    return call(
        functools.partial(query_back_kernel, seqs, lines),
        "query_back",
        outs,
        *dq_own,
        *dq_came,
        *own,
        *came,
        weight,
        prefetch=where,
        scratch=[pltpu.VMEM((width, own_width), F32)],
        flops=8 * seqs * local * width * own_width,
    )


def half_lanes(value):
    lane = lax.broadcasted_iota(jnp.int32, value.shape, 1)
    zero = jnp.zeros_like(value)
    return [jnp.where(lane < HD, value, zero), jnp.where(lane >= HD, value, zero)]


def half_rows(value):
    row = lax.broadcasted_iota(jnp.int32, value.shape, 0)
    zero = jnp.zeros_like(value)
    return [jnp.where(row < HD, value, zero), jnp.where(row >= HD, value, zero)]


def top_bits(value):
    spread = value * 65537.0
    return spread - (spread - value)


def in_three(value):
    first = top_bits(value)
    rest = value - first
    second = top_bits(rest)
    return first.astype(BF), second.astype(BF), (rest - second).astype(BF)


def packed_rows(values):
    terms = jnp.concatenate(in_three(values), axis=0)
    return jnp.concatenate([terms, jnp.zeros((16 - terms.shape[0], terms.shape[1]), BF)], axis=0)


def unpacked_rows(packed, count):
    packed = packed.astype(F32)
    return packed[:count] + packed[count : 2 * count] + packed[2 * count : 3 * count]


def below(shape, count):
    return lax.broadcasted_iota(jnp.int32, shape, 0) < count


def attend_kernel(slots, probe, old, counts, *refs):
    pieces = refs[: 2 * slots + 2]
    w_query, w_kv, b_query, b_kv = refs[2 * slots + 2 : 2 * slots + 6]
    queries, kv, o_own, packed, lse_ref, held, top, total, acc, heads = refs[2 * slots + 6 + old :]
    local = pieces[0].shape[0]
    rows = keys = 2 * local

    @pl.when(pl.program_id(0) == 0)
    def _():
        assemble(counts[slots + 1] == 1, pieces, held)

    scale = jnp.asarray(1.0 / math.sqrt(HD), BF)
    for start, to in ((0, 0), (slots * keys, rows)):
        query = (dot(held[start : start + rows, :], w_query[...], NN) + b_query[...]).astype(BF)
        queries[to : to + rows, :] = query * scale
    for h, query in enumerate(half_lanes(queries[...])):
        heads[h] = query

    @pl.loop(0, slots)
    def _(k):
        at = pl.ds(pl.multiple_of(k * keys, keys), keys)

        @pl.when(counts[k] > 0)
        def _():
            kv[at, :] = (dot(held[at, :], w_kv[...], NN) + b_kv[...]).astype(BF)

        @pl.when(counts[k] <= 0)
        def _():
            kv[at, :] = jnp.zeros((keys, 2 * PAIR), BF)

    def block(k):
        at = pl.ds(pl.multiple_of(k * keys, keys), keys)
        return kv[at, :PAIR], kv[at, PAIR:]

    first = pl.ds(pl.multiple_of(counts[slots] * keys, keys), probe)
    for h in range(2):
        top[h] = jnp.max(dot(kv[first, :PAIR], heads[h], NT), axis=0, keepdims=True)
    total[...] = jnp.zeros_like(total)
    acc[...] = jnp.zeros_like(acc)

    def quick(k, h, valid):
        key, value = block(k)
        expo = jnp.exp(dot(key, heads[h], NT) - top[h])
        if valid is not None:
            expo = jnp.where(below(expo.shape, valid), expo, 0.0)
        total[h] += jnp.sum(expo, axis=0, keepdims=True)
        acc[h] += dot(value, expo.astype(BF), TN)

    @pl.loop(0, slots)
    def _(k):
        valid = counts[k]

        @pl.when(valid >= keys)
        def _():
            quick(k, 0, None)
            quick(k, 1, None)

        @pl.when(jnp.logical_and(valid > 0, valid < keys))
        def _():
            pl.loop(0, 2)(lambda h: quick(k, h, valid))

    @pl.when(jnp.logical_not(jnp.max(total[...]) < LARGEST))
    def _():
        total[...] = jnp.zeros_like(total)
        acc[...] = jnp.zeros_like(acc)

        def careful(k, h, valid):
            key, value = block(k)
            scores = dot(key, heads[h], NT)
            scores = jnp.where(below(scores.shape, valid), scores, NEGATIVE)
            before = top[h]
            new = jnp.maximum(before, jnp.max(scores, axis=0, keepdims=True))
            expo = jnp.where(below(scores.shape, valid), jnp.exp(scores - new), 0.0)
            ratio = jnp.exp(before - new)
            total[h] = total[h] * ratio + jnp.sum(expo, axis=0, keepdims=True)
            acc[h] = acc[h] * ratio + dot(value, expo.astype(BF), TN)
            top[h] = new

        @pl.loop(0, slots)
        def _(k):
            valid = counts[k]

            @pl.when(valid > 0)
            def _():
                pl.loop(0, 2)(lambda h: careful(k, h, valid))

    lse = []
    for h in range(2):
        at = slice(h * HD, h * HD + HD)
        part = acc[h, at, :] / total[h]
        o_own[0, at, :] = part[:, :rows]
        packed[at, :] = part[:, rows:].astype(BF)
        lse.append(top[h] + jnp.log(total[h]))
        lse_ref[0, 0, h : h + 1, :] = lse[h][:, :rows]
    packed[PAIR:, :] = packed_rows(jnp.concatenate([l[:, rows:] for l in lse], axis=0))


def attend(counts, seqs, s, pieces, weights, before):
    w_query, w_kv, b_query, b_kv = weights
    slots = len(pieces) - 1
    local, model = pieces[0][0].shape
    rows, width = 2 * local, w_query.shape[1]
    pairs = width // PAIR
    keys = 2 * local
    total = width * 2 * rows * slots * keys
    anywhere = pl.BlockSpec(memory_space=pl.ANY)
    across = lambda p, c: (0, p)
    flat = [p for pair in pieces for p in pair]
    held = ((slots + 1) * keys, model)
    return pl.pallas_call(
        functools.partial(attend_kernel, slots, min(128, keys), len(before)),
        grid_spec=pltpu.PrefetchScalarGridSpec(
            num_scalar_prefetch=1,
            grid=(pairs,),
            in_specs=[pl.BlockSpec((local, model), lambda p, c: (0, 0), pipeline_mode=pl.Buffered(1)) for _ in flat]
            + [
                pl.BlockSpec((model, PAIR), across),
                pl.BlockSpec((model, 2 * PAIR), across),
                pl.BlockSpec((1, PAIR), across),
                pl.BlockSpec((1, 2 * PAIR), across),
            ]
            + [anywhere] * len(before),
            out_specs=[
                pl.BlockSpec((2 * rows, PAIR), across),
                pl.BlockSpec((slots * keys, 2 * PAIR), across),
                pl.BlockSpec((1, PAIR, rows), lambda p, c: (s, p, 0)),
                pl.BlockSpec((PAIR + 16, rows), lambda p, c: (p, 0)),
                pl.BlockSpec((1, 1, 2, rows), lambda p, c: (s, p, 0, 0)),
            ],
            scratch_shapes=[
                pltpu.VMEM(held, BF),
                pltpu.VMEM((2, 1, 2 * rows), F32),
                pltpu.VMEM((2, 1, 2 * rows), F32),
                pltpu.VMEM((2, PAIR, 2 * rows), F32),
                pltpu.VMEM((2, 2 * rows, PAIR), BF),
            ],
        ),
        out_shape=[
            jax.ShapeDtypeStruct((2 * rows, width), BF),
            jax.ShapeDtypeStruct((slots * keys, 2 * width), BF),
            jax.ShapeDtypeStruct((seqs, width, rows), F32),
            jax.ShapeDtypeStruct((pairs * (PAIR + 16), rows), BF),
            jax.ShapeDtypeStruct((seqs, pairs, 2, rows), F32),
        ],
        input_output_aliases={2 * slots + 7: 2, 2 * slots + 8: 4} if before else {},
        compiler_params=params(),
        cost_estimate=cost(16 * total, 2 * len(flat) * local * model + 8 * slots * keys * width, total // HD),
        name="attend",
    )(counts, *flat, *weights, *before)


def attend_back_kernel(slots, steps, split, first, counts, both, g_own, g_oth, kv, w_kv, *refs):
    pieces = refs[: 2 * slots]
    refs = refs[2 * slots :]
    if not first:
        before, bias_before = refs[:2]
        refs = refs[2:]
    dq_own, dq_oth, mine_ref, other_ref, bias_ref = refs[:5]
    weight_refs = refs[5:-8]
    acc, queries, grads, summed, facts, turned, part, d_weight = refs[-8:]
    rows = both.shape[0] // 2
    local = pieces[0].shape[0]
    keys = 2 * local
    step = pl.program_id(0)
    upper = counts[slots + 1] == 1

    @pl.when(step == 0)
    def _():
        part[...] = jnp.zeros_like(part)
        for k in range(slots):
            mine, came = pieces[2 * k][...], pieces[2 * k + 1][...]
            turned[:, 2 * k * local : (2 * k + 1) * local] = jnp.where(upper, came, mine).T
            turned[:, (2 * k + 1) * local : (2 * k + 2) * local] = jnp.where(upper, mine, came).T

    acc[...] = jnp.zeros_like(acc)
    d_weight[...] = jnp.zeros_like(d_weight) if first else before[...]
    bias_ref[...] = jnp.zeros_like(bias_ref) if first else bias_before[...]
    for block, g_ref in enumerate((g_own, g_oth)):
        stats = unpacked_rows(g_ref[PAIR:, :], 4)
        for h, (query, grad) in enumerate(
            zip(half_lanes(both[block * rows : block * rows + rows, :]), half_rows(g_ref[:PAIR, :]))
        ):
            queries[2 * block + h] = query
            grads[2 * block + h] = grad
            facts[2 * block + h, 0:1, :] = stats[h : h + 1]
            facts[2 * block + h, 1:2, :] = stats[2 + h : 3 + h]

    @pl.loop(0, slots)
    def _(k):
        valid = counts[k]
        rows_at = pl.ds(pl.multiple_of(k * keys, keys), keys)

        def one(at, valid):
            key, value = kv[rows_at, :PAIR], kv[rows_at, PAIR:]
            query, grad = queries[at], grads[at]
            prob = jnp.exp(dot(key, query, NT) - facts[at, 0:1, :])
            if valid is not None:
                prob = jnp.where(below(prob.shape, valid), prob, 0.0)
            change = dot(value, grad, NN) - facts[at, 1:2, :]
            score = (prob * change).astype(BF)
            summed[:, PAIR:] += dot(prob.astype(BF), grad, NT)
            summed[:, :PAIR] += dot(score, query, NN)
            acc[at] += dot(key, score, TN)

        summed[...] = jnp.zeros_like(summed)

        @pl.when(valid >= keys)
        def _():
            for at in range(4):
                one(at, None)

        @pl.when(jnp.logical_and(valid > 0, valid < keys))
        def _():
            pl.loop(0, 4)(lambda at: one(at, valid))

        @pl.when(valid > 0)
        def _():
            low = summed[...].astype(BF)
            part[rows_at, :] += dot(low, w_kv[...], NT)
            d_weight[...] += dot(turned[:, rows_at], low, NN)
            bias_ref[...] += jnp.sum(low.astype(F32), axis=0, keepdims=True)

    scale = 1.0 / math.sqrt(HD)
    for h in range(2):
        at = slice(h * HD, h * HD + HD)
        dq_own[at, :] = acc[h, at, :] * scale
        dq_oth[at, :] = (acc[2 + h, at, :] * scale).astype(BF)
    half = d_weight.shape[0] // 2
    if split:
        lower_line = counts[slots + 2] == 0
        low_half, high_half = d_weight[:half, :], d_weight[half:, :]
        weight_refs[0][...] = jnp.where(lower_line, low_half, high_half)
        weight_refs[1][...] = jnp.where(lower_line, high_half, low_half).astype(BF)
    else:
        weight_refs[0][...] = d_weight[...]

    @pl.when(step == steps - 1)
    def _():
        for k in range(slots):
            low = part[2 * k * local : (2 * k + 1) * local, :]
            high = part[(2 * k + 1) * local : (2 * k + 2) * local, :]
            to = slice(k * local, k * local + local)
            mine_ref[to, :] = jnp.where(upper, high, low).astype(BF)
            other_ref[to, :] = jnp.where(upper, low, high).astype(BF)


def attend_back(counts, both, g_own, g_oth, kv, w_kv, pieces, before, last):
    rows, width = both.shape[0] // 2, both.shape[1]
    pairs = width // PAIR
    slots = len(pieces)
    local, model = pieces[0][0].shape
    keys = 2 * local
    split = last and lax.axis_size("dp") == 2
    across = lambda p, c: (0, p)
    whole = lambda p, c: (0, 0)
    once = pl.Buffered(1)
    t_spec = pl.BlockSpec((PAIR, rows), lambda p, c: (p, 0))
    g_spec = pl.BlockSpec((PAIR + 16, rows), lambda p, c: (p, 0))
    flat = [p for pair in pieces for p in pair]
    extra = () if before is None else before
    if split:
        weight_outs = [((model // 2, 2 * width), F32), ((model // 2, 2 * width), BF)]
    else:
        weight_outs = [((model, 2 * width), F32)]
    total = width * 2 * rows * kv.shape[0]
    return pl.pallas_call(
        functools.partial(attend_back_kernel, slots, pairs, split, before is None),
        grid_spec=pltpu.PrefetchScalarGridSpec(
            num_scalar_prefetch=1,
            grid=(pairs,),
            in_specs=[
                pl.BlockSpec((2 * rows, PAIR), across),
                g_spec,
                g_spec,
                pl.BlockSpec((kv.shape[0], 2 * PAIR), across),
                pl.BlockSpec((model, 2 * PAIR), across),
            ]
            + [pl.BlockSpec((local, model), whole, pipeline_mode=once) for _ in flat]
            + [pl.BlockSpec((a.shape[0], 2 * PAIR), across) for a in extra],
            out_specs=[
                t_spec,
                t_spec,
                pl.BlockSpec((slots * local, model), whole, pipeline_mode=once),
                pl.BlockSpec((slots * local, model), whole, pipeline_mode=once),
                pl.BlockSpec((1, 2 * PAIR), across),
            ]
            + [pl.BlockSpec((shape[0], 2 * PAIR), across) for shape, _ in weight_outs],
            scratch_shapes=[
                pltpu.VMEM((4, PAIR, rows), F32),
                pltpu.VMEM((4, rows, PAIR), BF),
                pltpu.VMEM((4, PAIR, rows), BF),
                pltpu.VMEM((keys, 2 * PAIR), F32),
                pltpu.VMEM((4, 2, rows), F32),
                pltpu.VMEM((model, slots * keys), BF),
                pltpu.VMEM((slots * keys, model), F32),
                pltpu.VMEM((model, 2 * PAIR), F32),
            ],
        ),
        out_shape=[
            jax.ShapeDtypeStruct((width, rows), F32),
            jax.ShapeDtypeStruct((width, rows), BF),
            jax.ShapeDtypeStruct((slots * local, model), BF),
            jax.ShapeDtypeStruct((slots * local, model), BF),
            jax.ShapeDtypeStruct((1, 2 * width), F32),
        ]
        + [jax.ShapeDtypeStruct(shape, kind) for shape, kind in weight_outs],
        compiler_params=params(),
        cost_estimate=cost(40 * total, 8 * both.size + 4 * kv.size + 8 * len(flat) * local * model, total // HD),
        name="attend_back",
    )(counts, both, g_own, g_oth, kv, w_kv, *flat, *extra)


def merge_kernel(pairs, seqs, where, o_own, lse_own, *refs):
    packs = refs[:seqs]
    weight, full_ref, low_ref, mine_ref, other_ref, lse_ref, low_s, packed = refs[seqs:]
    rows = o_own.shape[2]
    for s in range(seqs):

        @pl.when(pl.program_id(0) == s)
        def _(s=s):
            packed[...] = packs[s][...]

    for p in range(pairs):
        base = p * (PAIR + 16)
        own = lse_own[0, p]
        came = unpacked_rows(packed[base + PAIR : base + PAIR + 16, :], 2)
        highest = jnp.maximum(own, came)
        share_own, share_came = jnp.exp(own - highest), jnp.exp(came - highest)
        both = share_own + share_came
        lse_ref[0, p] = highest + jnp.log(both)
        share_own, share_came = share_own / both, share_came / both
        for h in range(2):
            at = slice(p * PAIR + h * HD, p * PAIR + h * HD + HD)
            term = packed[base + h * HD : base + h * HD + HD, :].astype(F32)
            merged = o_own[0, at, :] * share_own[h : h + 1] + term * share_came[h : h + 1]
            full_ref[0, at, :] = merged
            low_s[at, :] = merged.astype(BF)
    low_ref[0] = low_s[...]
    half = rows // 2
    mine = pl.ds(pl.multiple_of(where[0] * half, half), half)
    other = pl.ds(pl.multiple_of((1 - where[0]) * half, half), half)
    dims = (((0,), (1,)), ((), ()))
    mine_ref[0] = dot(low_s[:, mine], weight[...], dims)
    other_ref[0] = dot(low_s[:, other], weight[...], dims).astype(BF)


def merge(where, o_own, lse_own, packs, weight):
    seqs, width, rows = o_own.shape
    pairs = width // PAIR
    model = weight.shape[0]
    one = lambda *shape: pl.BlockSpec((1, *shape), lambda s, w: (s,) + (0,) * len(shape))
    return pl.pallas_call(
        functools.partial(merge_kernel, pairs, seqs),
        grid_spec=pltpu.PrefetchScalarGridSpec(
            num_scalar_prefetch=1,
            grid=(seqs,),
            in_specs=[
                one(width, rows),
                one(pairs, 2, rows),
            ]
            + [pl.BlockSpec(p.shape, lambda s, w: (0, 0)) for p in packs]
            + [
                pl.BlockSpec(weight.shape, lambda s, w: (0, 0)),
            ],
            out_specs=[one(width, rows), one(width, rows), one(rows // 2, model), one(rows // 2, model), one(pairs, 2, rows)],
            scratch_shapes=[pltpu.VMEM((width, rows), BF), pltpu.VMEM(packs[0].shape, BF)],
        ),
        out_shape=[
            jax.ShapeDtypeStruct((seqs, width, rows), F32),
            jax.ShapeDtypeStruct((seqs, width, rows), BF),
            jax.ShapeDtypeStruct((seqs, rows // 2, model), F32),
            jax.ShapeDtypeStruct((seqs, rows // 2, model), BF),
            jax.ShapeDtypeStruct((seqs, pairs, 2, rows), F32),
        ],
        compiler_params=params(),
        cost_estimate=cost(2 * seqs * width * rows * model, 12 * o_own.size + 4 * seqs * rows * model),
        name="merge",
    )(where, o_own, lse_own, *packs, weight)


def turn_kernel(pairs, seqs, where, own_ref, came_ref, weight, full_ref, lse_ref, *refs):
    packs, packed = refs[:seqs], refs[-1]
    step = pl.program_id(0)
    upper = where[0] == 1
    own, came = own_ref[0], came_ref[0]
    rows = jnp.concatenate([jnp.where(upper, came, own), jnp.where(upper, own, came)], axis=0)
    grad = dot(weight[...], rows, (((0,), (1,)), ((), ()))).astype(BF)
    product = grad.astype(F32) * full_ref[0]
    for p in range(pairs):
        base = p * (PAIR + 16)
        packed[base : base + PAIR, :] = grad[p * PAIR : p * PAIR + PAIR]
        stats = [lse_ref[0, p]]
        for h in range(2):
            at = slice(p * PAIR + h * HD, p * PAIR + h * HD + HD)
            stats.append(jnp.sum(product[at], axis=0, keepdims=True))
        packed[base + PAIR : base + PAIR + 16, :] = packed_rows(jnp.concatenate(stats, axis=0))
    for s in range(seqs):

        @pl.when(step == s)
        def _(s=s):
            packs[s][...] = packed[...]


def output_kernel(seqs, lines, where, own_ref, came_ref, low_ref, *refs):
    weight_refs, d_weight = refs[:-1], refs[-1]
    step = pl.program_id(0)
    upper = where[0] == 1
    own, came = own_ref[0], came_ref[0]
    rows = jnp.concatenate([jnp.where(upper, came, own), jnp.where(upper, own, came)], axis=0)

    @pl.when(step == 0)
    def _():
        d_weight[...] = jnp.zeros_like(d_weight)

    d_weight[...] += dot(rows, low_ref[0], (((0,), (1,)), ((), ())))

    @pl.when(step == seqs - 1)
    def _():
        if lines == 2:
            kept, sent = own_rows(where[1], d_weight, d_weight.shape[0] // 2)
            weight_refs[0][...] = kept
            weight_refs[1][...] = sent.astype(BF)
        else:
            weight_refs[0][...] = d_weight[...]


def output_grad(where, own, came, low):
    seqs, width, rows = low.shape
    model = own.shape[2]
    lines = lax.axis_size("dp")
    one = lambda *shape: pl.BlockSpec((1, *shape), lambda s, w: (s,) + (0,) * len(shape))
    outs = [((model // 2, width), F32), ((model // 2, width), BF)] if lines == 2 else [((model, width), F32)]
    return pl.pallas_call(
        functools.partial(output_kernel, seqs, lines),
        grid_spec=pltpu.PrefetchScalarGridSpec(
            num_scalar_prefetch=1,
            grid=(seqs,),
            in_specs=[one(*own.shape[1:]), one(*own.shape[1:]), one(width, rows)],
            out_specs=[pl.BlockSpec(shape, lambda s, w: (0, 0)) for shape, _ in outs],
            scratch_shapes=[pltpu.VMEM((model, width), F32)],
        ),
        out_shape=[jax.ShapeDtypeStruct(shape, kind) for shape, kind in outs],
        compiler_params=params(),
        cost_estimate=cost(2 * seqs * rows * model * width, 4 * low.size + 4 * own.size),
        name="output_grad",
    )(where, own, came, low)


def turn(where, own, came, weight, full, lse):
    seqs, width, rows = full.shape
    pairs = width // PAIR
    one = lambda *shape: pl.BlockSpec((1, *shape), lambda s, w: (s,) + (0,) * len(shape))
    whole = lambda *shape: pl.BlockSpec(shape, lambda s, w: (0, 0))
    pack_shape = (pairs * (PAIR + 16), rows)
    return pl.pallas_call(
        functools.partial(turn_kernel, pairs, seqs),
        grid_spec=pltpu.PrefetchScalarGridSpec(
            num_scalar_prefetch=1,
            grid=(seqs,),
            in_specs=[
                one(*own.shape[1:]),
                one(*own.shape[1:]),
                whole(*weight.shape),
                one(width, rows),
                one(pairs, 2, rows),
            ],
            out_specs=[whole(*pack_shape)] * seqs,
            scratch_shapes=[pltpu.VMEM(pack_shape, BF)],
        ),
        out_shape=[jax.ShapeDtypeStruct(pack_shape, BF)] * seqs,
        compiler_params=params(),
        cost_estimate=cost(2 * seqs * rows * weight.size, 6 * full.size + 4 * own.size),
        name="turn",
    )(where, own, came, weight, full, lse)


def gelu_parts(u):
    density = jnp.exp(-0.5 * u * u)
    t = 1.0 / (1.0 + (0.3275911 / math.sqrt(2.0)) * jnp.abs(u))
    series = t * (
        0.254829592
        + t * (-0.284496736 + t * (1.421413741 + t * (-1.453152027 + t * 1.061405429)))
    )
    tail = 0.5 * series * density
    share = jnp.where(u < 0.0, tail, 1.0 - tail)
    return u * share, share + u * (density * (1.0 / math.sqrt(2.0 * math.pi)))


def feed_kernel(chunk, half, own_ref, came_ref, w_in, bias, w_out, active_ref, slope_ref, mine_ref, other_ref):
    step = pl.program_id(0)
    rows = jnp.where(step < half, own_ref[...], came_ref[...])
    part = None
    for start in range(0, w_in.shape[1], chunk):
        at = slice(start, start + chunk)
        inner = dot(rows, w_in[:, at], NN) + bias[:, at]
        active, slope = gelu_parts(inner)
        active = active.astype(BF)
        active_ref[:, at] = active
        slope_ref[:, at] = slope.astype(BF)
        term = dot(active, w_out[:, at], NT)
        part = term if part is None else part + term

    @pl.when(step < half)
    def _():
        mine_ref[...] = part

    @pl.when(step >= half)
    def _():
        other_ref[...] = part.astype(BF)


def row_specs(block, half, width):
    own = pl.BlockSpec((block, width), lambda i, *c: (jnp.minimum(i, half - 1), 0))
    came = pl.BlockSpec((block, width), lambda i, *c: (jnp.maximum(i - half, 0), 0))
    return own, came


def feed(own, came, w_in, bias, w_out):
    count, width = own.shape
    units = w_in.shape[1]
    block = min(FEED_ROWS, count)
    half = count // block
    whole = lambda i: (0, 0)
    by_row = lambda i: (i, 0)
    own_spec, came_spec = row_specs(block, half, width)
    return pl.pallas_call(
        functools.partial(feed_kernel, units // 3 if units % 384 == 0 else units, half),
        grid=(2 * half,),
        in_specs=[
            own_spec,
            came_spec,
            pl.BlockSpec((width, units), whole, pipeline_mode=pl.Buffered(1)),
            pl.BlockSpec((1, units), whole),
            pl.BlockSpec((width, units), whole, pipeline_mode=pl.Buffered(1)),
        ],
        out_specs=[pl.BlockSpec((block, units), by_row), pl.BlockSpec((block, units), by_row), own_spec, came_spec],
        out_shape=[
            jax.ShapeDtypeStruct((2 * count, units), BF),
            jax.ShapeDtypeStruct((2 * count, units), BF),
            jax.ShapeDtypeStruct((count, width), F32),
            jax.ShapeDtypeStruct((count, width), BF),
        ],
        compiler_params=params(),
        cost_estimate=cost(8 * count * width * units, 4 * width * units + 8 * count * units + 12 * count * width, 2 * count * units),
        name="feed",
    )(own, came, w_in, bias, w_out)


def feed_back_kernel(half, lines, where, low_own, low_came, own_ref, came_ref, active_ref, slope_ref, w_in, w_out, *refs):
    mine_ref, other_ref, d_bias_ref = refs[:3]
    weight_refs, (d_in, d_out) = refs[3:-2], refs[-2:]
    step = pl.program_id(0)
    units = w_in.shape[1]

    @pl.when(step == 0)
    def _():
        d_in[...] = jnp.zeros_like(d_in)
        d_out[...] = jnp.zeros_like(d_out)
        d_bias_ref[...] = jnp.zeros_like(d_bias_ref)

    low = jnp.where(step < half, low_own[...], low_came[...])
    rows = jnp.where(step < half, own_ref[...], came_ref[...])
    inner = (dot(low, w_out[...], NN) * slope_ref[...].astype(F32)).astype(BF)
    part = dot(inner, w_in[...], NT)
    d_out[...] += dot(low, active_ref[...], TN)
    d_in[...] += dot(rows, inner, TN)
    d_bias_ref[...] += jnp.sum(inner.astype(F32), axis=0, keepdims=True)

    @pl.when(step < half)
    def _():
        mine_ref[...] = part

    @pl.when(step >= half)
    def _():
        other_ref[...] = part.astype(BF)

    @pl.when(step == 2 * half - 1)
    def _():
        for total, cut in ((d_in, slice(0, units)), (d_out, slice(units, 2 * units))):
            if lines == 2:
                kept, sent = own_rows(where[1], total, total.shape[0] // 2)
                weight_refs[0][:, cut] = kept.astype(BF)
                weight_refs[1][:, cut] = sent.astype(BF)
            else:
                weight_refs[0][:, cut] = total[...].astype(BF)


def feed_back(where, low_own, low_came, own, came, active, slope, w_in, w_out):
    count, width = own.shape
    units = w_in.shape[1]
    block = min(FEED_ROWS, count)
    half = count // block
    whole = lambda i, *c: (0, 0)
    by_row = lambda i, *c: (i, 0)
    once = pl.Buffered(1)
    lines = lax.axis_size("dp")
    own_spec, came_spec = row_specs(block, half, width)
    d_shape = (width // 2 if lines == 2 else width, 2 * units)
    d_count = 2 if lines == 2 else 1
    return pl.pallas_call(
        functools.partial(feed_back_kernel, half, lines),
        grid_spec=pltpu.PrefetchScalarGridSpec(
            num_scalar_prefetch=1,
            grid=(2 * half,),
            in_specs=[
                own_spec,
                came_spec,
                own_spec,
                came_spec,
                pl.BlockSpec((block, units), by_row),
                pl.BlockSpec((block, units), by_row),
                pl.BlockSpec((width, units), whole, pipeline_mode=once),
                pl.BlockSpec((width, units), whole, pipeline_mode=once),
            ],
            out_specs=[own_spec, came_spec, pl.BlockSpec((1, units), whole)]
            + [pl.BlockSpec(d_shape, whole, pipeline_mode=once)] * d_count,
            scratch_shapes=[pltpu.VMEM((width, units), F32), pltpu.VMEM((width, units), F32)],
        ),
        out_shape=[
            jax.ShapeDtypeStruct((count, width), F32),
            jax.ShapeDtypeStruct((count, width), BF),
            jax.ShapeDtypeStruct((1, units), F32),
        ]
        + [jax.ShapeDtypeStruct(d_shape, BF)] * d_count,
        compiler_params=params(),
        cost_estimate=cost(16 * count * width * units, 8 * width * units + 8 * count * units + 16 * count * width),
        name="feed_back",
    )(where, low_own, low_came, own, came, active, slope, w_in, w_out)


def centre(values):
    middle = values - jnp.mean(values, axis=-1, keepdims=True)
    scale = lax.rsqrt(jnp.mean(middle * middle, axis=-1, keepdims=True) + EPSILON)
    return middle * scale, scale


def back_through(weighted, normal, scale):
    first = jnp.mean(weighted, axis=-1, keepdims=True)
    second = jnp.mean(weighted * normal, axis=-1, keepdims=True)
    return (weighted - first - normal * second) * scale


def first_kernel(x_ref, mine_ref, came_ref, vec_ref, normal_ref, scale_ref, low_ref):
    sums = x_ref[...].astype(F32) + (mine_ref[...] + came_ref[...].astype(F32)) + vec_ref[0:1, :]
    normal, scale = centre(sums)
    normal_ref[...] = normal
    scale_ref[...] = scale
    low_ref[...] = (normal * vec_ref[1:2, :] + vec_ref[2:3, :]).astype(BF)


def second_kernel(per_seq, counts, normal_ref, mine_ref, came_ref, cot_ref, vec_ref, out_ref, grad_ref, low_ref, sums_ref):
    step = pl.program_id(0)
    block = normal_ref.shape[0]
    valid = counts[step // per_seq] - (step % per_seq) * block
    keep = lax.broadcasted_iota(jnp.int32, normal_ref.shape, 0) < valid

    @pl.when(step == 0)
    def _():
        sums_ref[...] = jnp.zeros_like(sums_ref)

    first = normal_ref[...] * vec_ref[1:2, :] + vec_ref[2:3, :]
    sums = first + (mine_ref[...] + came_ref[...].astype(F32)) + vec_ref[3:4, :]
    normal, scale = centre(sums)
    out_ref[...] = jnp.where(keep, normal * vec_ref[4:5, :] + vec_ref[5:6, :], 0.0)
    out_grad = jnp.where(keep, cot_ref[...].astype(F32), 0.0)
    grad = back_through(out_grad * vec_ref[4:5, :], normal, scale)
    grad_ref[...] = grad
    low_ref[...] = grad.astype(BF)
    sums_ref[0:1, :] += jnp.sum(out_grad * normal, axis=0, keepdims=True)
    sums_ref[1:2, :] += jnp.sum(out_grad, axis=0, keepdims=True)
    sums_ref[2:3, :] += jnp.sum(grad, axis=0, keepdims=True)


def first_back_kernel(grad_ref, mine_ref, came_ref, normal_ref, scale_ref, vec_ref, out_ref, low_ref, sums_ref):
    @pl.when(pl.program_id(0) == 0)
    def _():
        sums_ref[...] = jnp.zeros_like(sums_ref)

    given = grad_ref[...] + (mine_ref[...] + came_ref[...].astype(F32))
    normal = normal_ref[...]
    grad = back_through(given * vec_ref[1:2, :], normal, scale_ref[...])
    out_ref[...] = grad
    low_ref[...] = grad.astype(BF)
    sums_ref[0:1, :] += jnp.sum(given * normal, axis=0, keepdims=True)
    sums_ref[1:2, :] += jnp.sum(given, axis=0, keepdims=True)
    sums_ref[2:3, :] += jnp.sum(grad, axis=0, keepdims=True)


def row_call(kernel, name, block, count, width, inputs, whole_inputs, outs, sums, counts=None):
    by_row = lambda i, *c: (i, 0)
    whole = lambda i, *c: (0, 0)
    in_specs = [pl.BlockSpec((block, a.shape[1]), by_row) for a in inputs]
    in_specs += [pl.BlockSpec(a.shape, whole) for a in whole_inputs]
    out_specs = [pl.BlockSpec((block, w), by_row) for w, _ in outs]
    out_shape = [jax.ShapeDtypeStruct((count, w), t) for w, t in outs]
    if sums:
        out_specs.append(pl.BlockSpec((8, width), whole))
        out_shape.append(jax.ShapeDtypeStruct((8, width), F32))
    prefetch = 0 if counts is None else 1
    moved = sum(a.size * a.dtype.itemsize for a in inputs) + sum(count * w * 4 for w, _ in outs)
    return pl.pallas_call(
        kernel,
        grid_spec=pltpu.PrefetchScalarGridSpec(
            num_scalar_prefetch=prefetch, grid=(count // block,), in_specs=in_specs, out_specs=out_specs
        ),
        out_shape=out_shape,
        compiler_params=params(),
        cost_estimate=cost(20 * count * width, moved),
        name=name,
    )(*(() if counts is None else (counts,)), *inputs, *whole_inputs)


def interleaved(key, value):
    width = key.shape[1]
    pieces = []
    for start in range(0, width, PAIR):
        pieces += [key[:, start : start + PAIR], value[:, start : start + PAIR]]
    return jnp.concatenate(pieces, axis=1)


def apart(both):
    keys, values = [], []
    for start in range(0, both.shape[1], 2 * PAIR):
        keys.append(both[:, start : start + PAIR])
        values.append(both[:, start + PAIR : start + 2 * PAIR])
    return jnp.concatenate(keys, axis=1), jnp.concatenate(values, axis=1)


def on_device(
    block_input,
    lengths,
    cotangent,
    query_weight,
    query_bias,
    key_weight,
    value_weight,
    value_bias,
    output_weight,
    output_bias,
    first_gain,
    first_shift,
    inner_weight,
    inner_bias,
    outer_weight,
    closing_offset_vector,
    second_gain,
    second_shift,
):
    seqs, local, width = block_input.shape
    chip = 2 * local
    spots = lax.axis_size("ctx")
    spot = lax.axis_index("ctx")
    part = lax.axis_index("tp")
    core, side = part % 2, part // 2
    is_upper_core, is_upper_side = core == 1, side == 1
    span = local * lax.axis_size("tp")
    heads_width = query_weight.shape[1]
    unit_width = inner_weight.shape[1]
    count = seqs * local

    def other_core(value, **ties):
        return swap(value, "tp", 1, **ties)

    def other_side(value, **ties):
        return swap(value, "tp", 2, **ties)

    def flat(value):
        return value.reshape(-1, value.shape[-1])

    starts = jnp.stack([(spot ^ k) * span + side * chip for k in range(spots)])
    key_counts = jnp.clip(lengths[:, None] - starts[None, :], 0, chip)
    facts = jnp.stack([spot, core, lax.axis_index("dp")]).astype(jnp.int32)
    counts = jnp.concatenate([key_counts.astype(jnp.int32), jnp.broadcast_to(facts, (seqs, 3))], axis=1)
    row_counts = jnp.clip(lengths - (spot * span + part * local), 0, local).astype(jnp.int32)
    where = jnp.stack([core, lax.axis_index("dp")]).astype(jnp.int32)

    def together(*values):
        return lax.optimization_barrier(values)

    def over_spots(value, done=()):
        return [swap(value, "ctx", k, (), done) for k in range(1, spots)]

    lines = lax.axis_size("dp")
    own_width = 2 * heads_width
    attention_shard = pack([[(query_weight, False), (key_weight, False), (value_weight, False)]])
    biases = jnp.concatenate([query_bias, value_bias, inner_bias])[None, :]
    x_rows = [block_input[s] for s in range(seqs)]

    def send_near(own):
        return [swap(own, "ctx", 2), swap(own, "ctx", 1)] if spots == 4 else over_spots(own)

    def send_last(own, far):
        return [
            lax.ppermute(own, "ctx", [(1, 2), (2, 1)]),
            lax.ppermute(far, "ctx", [(2, 3), (1, 0)]),
        ]

    def finish(nears, lasts):
        if spots != 4:
            return nears
        in_middle = jnp.logical_or(spot == 1, spot == 2)
        return [nears[1], nears[0], jnp.where(in_middle, lasts[0], lasts[1])]

    came, across, *near = together(other_core(block_input), other_side(block_input), *over_spots(attention_shard))
    first_out = after(x_rows[0], *near)
    (attention_near,) = stack([attention_shard, *near])
    diagonal = [(d * 4 + t, (1 - d) * 4 + (t ^ 2)) for d in range(2) for t in range(4)]
    over_both = [lax.ppermute(attention_near, ("dp", "tp"), diagonal)] if lines == 2 else []
    attention_other, attention_line, *nears = together(
        other_side(attention_near), swap(attention_near, "dp", 1), *over_both, *send_near(first_out)
    )
    if lines == 2:
        other_line, *nears = nears
    cores = [other_core(n) for n in nears]
    lasts = send_last(after(x_rows[0], *nears), nears[0]) if spots == 4 else []
    biases_came = other_side(after(biases, *nears))
    biases_came, *rest = together(biases_came, *lasts, *cores)
    lasts, cores = rest[: len(lasts)], rest[len(lasts) :]
    arrived = [finish(nears, lasts)]
    if spots == 4:
        cores = [cores[1], cores[0], other_core(arrived[0][2])]
    if lines == 2:
        attention_all = [[attention_near, attention_other], [attention_line, other_line]]
    else:
        attention_all = over_dp([attention_near, attention_other])
    query_full, kv_full = place(attention_all, [heads_width] * 3, [(0,), (1, 2)])

    query_b = ordered(biases[:, :heads_width], biases_came[:, :heads_width], is_upper_side, 1)
    cut = slice(heads_width, own_width)
    value_b = ordered(biases[:, cut], biases_came[:, cut], is_upper_side, 1)
    cut = slice(own_width, None)
    inner_b = ordered(biases[:, cut], biases_came[:, cut], is_upper_side, 1)
    kv_bias = interleaved(jnp.zeros_like(value_b), value_b)

    pieces = [[(x_rows[0], came[0])] + list(zip(arrived[0], cores))]
    across_core = other_core(across[0])
    late_weights = together(output_weight, inner_weight, outer_weight, *nears)
    feed_shard = pack([[(late_weights[0], True), (late_weights[1], False)], [(late_weights[2], True)]])
    feed_shard = after(feed_shard, arrived[0][-1])
    feed_near = over_spots(feed_shard)
    second_nears = send_near(after(x_rows[1], arrived[0][-1]))
    weights = (query_full, kv_full, query_b, kv_bias)
    q, made, own, packed, lse = attend(counts[0], seqs, 0, pieces[0] + [(across[0], across_core)], weights, ())
    queries, kv = [q], [made]
    packs = [packed]

    own, *feed_near = together(own, *feed_near)
    near_a, near_b = stack([feed_shard] + feed_near, feed_shard.shape[1] - unit_width - -unit_width % 128)
    sending_a, sending_b = other_side(near_a), swap(near_b, "dp", 1)
    nears = together(near_a, *second_nears)[1:]
    across_core = other_core(across[1])
    cores = [other_core(n) for n in nears]
    lasts = send_last(after(x_rows[1], own), nears[0]) if spots == 4 else []
    other_a, line_b, *rest = together(sending_a, sending_b, *lasts, *cores)
    packs[0] = other_side(after(packs[0], other_a))
    lasts, cores = rest[: len(lasts)], rest[len(lasts) :]
    arrived.append(finish(nears, lasts))
    if spots == 4:
        cores = [cores[1], cores[0], other_core(arrived[1][2])]
    pieces.append([(x_rows[1], came[1])] + list(zip(arrived[1], cores)))
    if lines == 2:
        last_b = [near_b, line_b]
        sent_a = [swap(after(a, line_b), "dp", 1) for a in (near_a, other_a)]
        sent_b = [other_side(after(b, other_a)) for b in last_b]
    q, made, own, packed, lse = attend(counts[1], seqs, 1, pieces[1] + [(across[1], across_core)], weights, (own, lse))
    queries.append(q)
    kv.append(made)
    buffers = (own, lse)
    packs.append(other_side(packed))
    if lines == 2:
        sent = together(*sent_a, *sent_b, own)
        sent_a, sent_b = list(sent[:2]), list(sent[2:4])
        all_a = [[near_a, other_a], sent_a]
        all_b = [[near_b, sent_b[0]], [line_b, sent_b[1]]]
    else:
        all_a, all_b = over_dp([near_a, other_a]), over_dp([near_b, other_side(near_b)])
    output_full, inner_full = place(all_a, [heads_width, unit_width], [(0,), (1,)])
    (outer_full,) = place(all_b, [unit_width], [(0,)])

    vectors = jnp.stack([output_bias, first_gain, first_shift, closing_offset_vector, second_gain, second_shift])
    vectors = jnp.concatenate([vectors, jnp.zeros((2, width), F32)])
    block = local

    attended, attended_low, mine, other, lse_all = merge(where, *buffers, packs, output_full)
    normal, spread, first_low = row_call(
        first_kernel,
        "first_norm",
        block,
        count,
        width,
        [flat(block_input), flat(mine), flat(other_core(other))],
        [vectors],
        [(width, F32), (1, F32), (width, BF)],
        False,
    )
    first_came = other_core(first_low)
    active, slope, mine, other = feed(first_low, first_came, inner_full, inner_b, outer_full)
    output, second_grad, outer_low, second_sums = row_call(
        functools.partial(second_kernel, local // block),
        "second_norm",
        block,
        count,
        width,
        [normal, mine, other_core(other), flat(cotangent)],
        [vectors],
        [(width, F32), (width, F32), (width, BF)],
        True,
        row_counts,
    )
    mine, other, d_inner_bias, *d_feed = feed_back(
        where, outer_low, other_core(outer_low), first_low, first_came, active, slope, inner_full, outer_full
    )
    first_grad, attn_low, first_sums = row_call(
        first_back_kernel,
        "first_norm_back",
        block,
        count,
        width,
        [second_grad, mine, other_core(other), normal, spread],
        [vectors],
        [(width, F32), (width, BF)],
        True,
    )
    attn_low = attn_low.reshape(seqs, local, width)
    attn_came = other_core(attn_low)
    g_own = turn(where, attn_low, attn_came, output_full, attended, lse_all)
    d_output = output_grad(where, after(attn_low, *g_own), attn_came, attended_low)
    g_oth = [other_side(g) for g in g_own]

    lines = lax.axis_size("dp")

    def over_lines(made, done=()):
        if lines == 2:
            return made[0], swap(made[1], "dp", 1, (), done)
        value, place_at = made[0].astype(F32), lax.axis_index("dp")
        for bit in reversed(bits_of("dp")):
            mine, sent = halves(value, (place_at & bit) != 0, 0)
            term = swap(sent.astype(BF), "dp", bit, (), done)
            value = mine + term.astype(F32)
        return mine, term

    def sides_of(pair, width_of_side):
        return [(pair, 0, width_of_side)], [(pair, width_of_side, width_of_side)]

    def back(s, g_in, before):
        return attend_back(
            counts[s], queries[s], g_own[s], g_in, kv[s], kv_full, pieces[s], before, s == seqs - 1
        )

    def by_spot(mine, came):
        total = (mine.astype(F32) + came.astype(F32)).reshape(spots, local, width)
        return total[0], [total[k].astype(BF) for k in range(1, spots)]

    shared = jnp.concatenate([second_sums[:3], first_sums[:3]])
    shared_came = other_core(shared)
    output_mine, output_came = over_lines(d_output)
    g_in, shared_came = together(g_oth[0], shared_came)
    early = jnp.concatenate([(shared + shared_came).reshape(1, -1), d_inner_bias], axis=1)
    early_near = swap(early, "ctx", 1)
    own, oth, mine, other, kv_bias_sum, *kv_grads = back(0, g_in, None)
    dq_own = [own]
    oth, other, g_oth[1], output_came, early_near = together(oth, other, g_oth[1], output_came, early_near)
    output_pair = (output_mine, output_came)
    dq_came_0 = other_side(oth)
    kept_0, sent_0 = by_spot(mine, other_core(other))
    early = early + early_near
    early_far = [swap(early, "ctx", bit) for bit in bits_of("ctx")[1:]]
    feed_pairs = [over_lines(d_feed, (kv_bias_sum,))]
    feed_kept, feed_sent = fold_sides(
        feed_pairs,
        [
            sides_of(0, unit_width),
            ([(0, 2 * unit_width, unit_width)], [(0, 3 * unit_width, unit_width)]),
        ],
        BF,
    )
    feed_term = other_side(feed_sent)
    came_0 = [swap(t, "ctx", k + 1) for k, t in enumerate(sent_0)]
    g_in, dq_came_0, early, *rest = together(g_oth[1], dq_came_0, early, *early_far, feed_sent, *sent_0)
    early = sum(rest[: len(early_far)], early)
    own, oth, mine, other, kv_bias_sum, *kv_grads = back(1, g_in, (kv_grads[0], kv_bias_sum))
    dq_own.append(own)

    oth, other, feed_term, *rest = together(oth, other, feed_term, *came_0, *kv_grads)
    came_0, kv_grads = rest[: spots - 1], rest[spots - 1 :]
    dq_came_1 = other_side(oth)
    kept_1, sent_1 = by_spot(mine, other_core(other))
    feed_all_rows = add_low(feed_kept, feed_term)
    feed_spread = lax.all_to_all(feed_all_rows, "ctx", split_axis=0, concat_axis=0, tiled=True)
    dq_came = [dq_came_0, after(dq_came_1, feed_all_rows, *sent_1)]
    kv_pair = over_lines(kv_grads)
    mine, other, query_bias_sum, *query_grads = query_back(
        where, dq_own, dq_came, x_rows, [came[s] for s in range(seqs)], query_full
    )
    query_term = (mine + other_core(other).astype(F32)).reshape(seqs, local, width)
    query_pair = over_lines(query_grads)
    value_bias_sum = apart(kv_bias_sum)[1]
    vector = jnp.concatenate([early, query_bias_sum.reshape(1, -1), value_bias_sum], axis=1)
    for bit in bits_of("dp"):
        vector = vector + swap(vector, "dp", bit)
    if spots == 4:
        near_1, far_1, last_1 = sent_1
        first_1 = [
            lax.ppermute(last_1, "ctx", [(3, 2), (0, 1)]),
            lax.ppermute(last_1, "ctx", [(1, 2), (2, 1)]),
        ]
    else:
        first_1 = [swap(sent_1[0], "ctx", 1)]
    if lines == 2:
        query_last, kv_last, vector, *first_1 = together(query_pair[1], kv_pair[1], vector, *first_1)
        query_pair, kv_pair = (query_pair[0], query_last), (kv_pair[0], kv_last)
    if spots == 4:
        passed, middle = first_1
        far_1 = (far_1.astype(F32) + passed.astype(F32)).astype(BF)
        came_1 = [middle, swap(far_1, "ctx", 2), swap(near_1, "ctx", 1)]
        query_pair = (query_pair[0], after(query_pair[1], far_1))
    else:
        came_1 = first_1 + [swap(t, "ctx", k + 2) for k, t in enumerate(sent_1[1:])]

    def side_cuts(pair, offset):
        cuts = []
        for start in (0, heads_width):
            pieces_of, at = [], start
            while at < start + heads_width:
                w = min(PAIR - at % PAIR, start + heads_width - at)
                pieces_of.append((pair, 2 * (at - at % PAIR) + offset + at % PAIR, w))
                at += w
            cuts.append(pieces_of)
        return tuple(cuts)

    kept, sent = fold_sides(
        [query_pair, kv_pair, output_pair],
        [sides_of(0, heads_width), side_cuts(1, 0), side_cuts(1, PAIR), sides_of(2, heads_width)],
    )
    vector_came = other_side(vector)
    term, feed_spread, vector_came, *rest = together(other_side(sent), feed_spread, vector_came, *came_1[1:])
    came_1[1:] = rest
    vector = vector + vector_came
    early, vector = vector[:, : early.shape[1]], vector[:, early.shape[1] :]
    spare = -vector.shape[1] % kept.shape[1]
    vector = jnp.pad(vector, ((0, 0), (0, spare))).reshape(-1, kept.shape[1])
    rows = fold_spots(kept, term, vector)
    terms = [swap(t, "ctx", k + 1) for k, t in enumerate(rows[1:])]
    feed_owned = jnp.sum(feed_spread.reshape(spots, -1, feed_spread.shape[1]).astype(F32), axis=0)
    size = rows[0].shape[0]
    owned = rows[0] + sum(t[:size].astype(F32) for t in terms)
    vector = (vector + sum(unpacked_rows(t[size:], vector.shape[0]) for t in terms)).reshape(-1)
    first_grad = first_grad.reshape(seqs, local, width)
    input_grad = jnp.stack(
        [
            first_grad[s] + query_term[s] + kept + sum(t.astype(F32) for t in came)
            for s, (kept, came) in enumerate(((kept_0, came_0), (kept_1, came_1)))
        ]
    )

    early = early[0]
    shared = early[: 6 * width].reshape(6, width)

    def own_side(value, start, size):
        return jnp.where(is_upper_side, value[start + size : start + 2 * size], value[start : start + size])

    return (
        output.reshape(seqs, local, width),
        input_grad,
        owned[:, :heads_width],
        own_side(vector, 0, heads_width),
        owned[:, heads_width:own_width],
        owned[:, own_width : own_width + heads_width],
        own_side(vector, own_width, heads_width),
        owned[:, 3 * heads_width : 4 * heads_width].T,
        shared[5],
        shared[3],
        shared[4],
        feed_owned[:, :unit_width],
        own_side(early, 6 * width, unit_width),
        feed_owned[:, unit_width : 2 * unit_width].T,
        shared[2],
        shared[0],
        shared[1],
    )


def solution(mesh):
    rows = P("dp", ("ctx", "tp"), None)
    into = P(("dp", "ctx"), "tp")
    out_of = P("tp", ("dp", "ctx"))
    split, whole = P("tp"), P()
    return jax.shard_map(
        on_device,
        mesh=mesh,
        in_specs=(
            rows, P("dp"), rows, into, split, into, into, split, out_of, whole, whole, whole,
            into, split, out_of, whole, whole, whole,
        ),
        out_specs=(
            rows, rows, into, split, into, into, split, out_of, whole, whole, whole,
            into, split, out_of, whole, whole, whole,
        ),
        check_vma=False,
    )
```

profile of v0, /device:TPU:0, one launch (start us, length us, event | category | flops | bytes accessed | tf_op | source)
XLA Modules:
  0.0 482.3 jit_solution(6591097381773531692)
XLA Ops:
  1.2 2.6 collective-permute-start.1
  5.5 3.6 collective-permute-start.4
  13.8 6.2 %collective-permute-done.3.refs_2_ = bf16[96,640]{1,0:T(8,128)(2,1)S(1)} collective-permute-done((bf16[96,640]{1,0:T(8,128)(2,1)}, bf16[96,640]{1,0:T(8,128)(2,1)S(1)}, u32[]{:S(2)}, u32[]{:S(2)}) %collective-permute-start.3) | collective-permute-done | bytes 122912 | tf_op jit(solution)/shard_map/ppermute | solution.py:46
  20.1 2.1 collective-permute-done.1
  22.2 1.9 stack.98.refs_0_
  24.1 2.7 collective-permute-start.7
  29.5 2.6 collective-permute-start.8
  32.7 13.5 %collective-permute-done.9.refs_2_ = bf16[256,768]{1,0:T(8,128)(2,1)} collective-permute-done((bf16[256,768]{1,0:T(8,128)(2,1)S(1)}, bf16[256,768]{1,0:T(8,128)(2,1)}, u32[]{:S(2)}, u32[]{:S(2)}) %collective-permute-start.9) | collective-permute-done | bytes 393248 | tf_op jit(solution)/shard_map/ppermute | solution.py:46
  46.2 2.4 collective-permute-done.8.refs_4_
  55.3 2.0 copy.39.refs_2_
  57.4 2.1 pack.3.refs_0_
  59.4 3.9 place.3
  64.5 3.7 collective-permute-start.19
  68.2 4.4 collective-permute-start.18
  73.5 2.1 collective-permute-start.21
  76.4 29.0 %attend.2 = (bf16[1024,384]{1,0:T(8,128)(2,1)}, bf16[2048,768]{1,0:T(8,128)(2,1)}, f32[2,384,512]{2,1,0:T(8,128)}, bf16[432,512]{1,0:T(8,128)(2,1)}, f32[2,3,2,512]{3,2,1,0:T(2,128)}) custom-call(s32[7]{0:T(128)} %get-tuple-element.386.counts, bf16[256,768]{1,0:T(8,128)(2,1)} %copy-done.2, bf16[256,768]{1,0:T(8,128)(2,1)} %get-tuple-element.367.refs_1_.refs_6_, ...), custom_call_target="tpu_custom_call" | custom-call | flops 12884901888 | bytes 10223616 | tf_op jit(solution)/shard_map/attend/pallas_call | solution.py:483
  106.4 2.5 stack.99
  109.8 6.2 %collective-permute-done.20.refs_4_ = bf16[256,768]{1,0:T(8,128)(2,1)S(1)} collective-permute-done((bf16[256,768]{1,0:T(8,128)(2,1)S(1)}, bf16[256,768]{1,0:T(8,128)(2,1)S(1)}, u32[]{:S(2)}, u32[]{:S(2)}) %collective-permute-start.20) | collective-permute-done | bytes 393248 | tf_op jit(solution)/shard_map/ppermute | solution.py:46
  118.3 17.5 %collective-permute-done.25 = bf16[256,768]{1,0:T(8,128)(2,1)S(1)} collective-permute-done((bf16[256,768]{1,0:T(8,128)(2,1)S(1)}, bf16[256,768]{1,0:T(8,128)(2,1)S(1)}, u32[]{:S(2)}, u32[]{:S(2)}) %collective-permute-start.25) | collective-permute-done | bytes 393248 | tf_op jit(solution)/shard_map/ppermute | solution.py:1168
  140.7 13.5 %attend.3 = (bf16[1024,384]{1,0:T(8,128)(2,1)}, bf16[2048,768]{1,0:T(8,128)(2,1)}, f32[2,384,512]{2,1,0:T(8,128)}, bf16[432,512]{1,0:T(8,128)(2,1)}, f32[2,3,2,512]{3,2,1,0:T(2,128)}) custom-call(s32[7]{0:T(128)} %get-tuple-element.387.counts, bf16[256,768]{1,0:T(8,128)(2,1)} %copy-done.3, ...), custom_call_target="tpu_custom_call", output_to_operand_aliasing={{2}: (15, {}), {4}: (16, {})} | custom-call | flops 12884901888 | bytes 10223616 | tf_op jit(solution)/shard_map/attend/pallas_call | solution.py:483
  154.3 7.3 %collective-permute-done.34.refs_1_ = bf16[384,768]{1,0:T(8,128)(2,1)S(1)} collective-permute-done((bf16[384,768]{1,0:T(8,128)(2,1)}, bf16[384,768]{1,0:T(8,128)(2,1)S(1)}, u32[]{:S(2)}, u32[]{:S(2)}) %collective-permute-start.34) | collective-permute-done | bytes 589856 | tf_op jit(solution)/shard_map/ppermute | solution.py:46
  162.6 11.6 %collective-permute-done.35.refs_3_ = bf16[384,768]{1,0:T(8,128)(2,1)S(1)} collective-permute-done((bf16[384,768]{1,0:T(8,128)(2,1)S(1)}, bf16[384,768]{1,0:T(8,128)(2,1)S(1)}, u32[]{:S(2)}, u32[]{:S(2)}) %collective-permute-start.35) | collective-permute-done | bytes 589856 | tf_op jit(solution)/shard_map/ppermute | solution.py:46
  175.6 4.9 %place.4 = (bf16[768,384]{1,0:T(8,128)(2,1)}, bf16[768,1536]{1,0:T(8,128)(2,1)}) custom-call(s32[3]{0:T(128)} %get-tuple-element.389.where, bf16[384,1024]{1,0:T(8,128)(2,1)} %get-tuple-element.212.refs_0_, bf16[384,1024]{1,0:T(8,128)(2,1)} %copy-done.12, bf16[384,1024]{1,0:T(8,128)(2,1)} %copy-done.13, bf16[384,1024]{1,0:T(8,128)(2,1)} %copy-done.14), custom_call_target="tpu_custom_call" | custom-call | bytes 9043968 | tf_op jit(solution)/shard_map/place/pallas_call | solution.py:68
  180.5 2.7 collective-permute-done.31.refs_1_
  184.0 5.1 %merge.1 = (f32[2,384,512]{2,1,0:T(8,128)}, bf16[2,384,512]{2,1,0:T(8,128)(2,1)}, f32[2,256,768]{2,1,0:T(8,128)}, bf16[2,256,768]{2,1,0:T(8,128)(2,1)}, f32[2,3,2,512]{3,2,1,0:T(2,128)}) custom-call(s32[2]{0:T(128)} %pad_add_fusion.1.where, f32[2,384,512]{2,1,0:T(8,128)} %get-tuple-element.205.o_own, f32[2,3,2,512]{3,2,1,0:T(2,128)} %get-tuple-element.206.lse_own, ...), custom_call_target="tpu_custom_call" | custom-call | flops 603979776 | bytes 7864320 | tf_op jit(solution)/shard_map/merge/pallas_call | solution.py:725
  192.4 3.4 first_norm.1
  196.7 3.8 place.5.w_out
  201.4 14.2 %feed.1 = (bf16[1024,1536]{1,0:T(8,128)(2,1)}, bf16[1024,1536]{1,0:T(8,128)(2,1)}, f32[512,768]{1,0:T(8,128)}, bf16[512,768]{1,0:T(8,128)(2,1)}) custom-call(bf16[512,768]{1,0:T(8,128)(2,1)} %get-tuple-element.222.own_ref, bf16[512,768]{1,0:T(8,128)(2,1)} %copy-done.59, bf16[768,1536]{1,0:T(8,128)(2,1)} %get-tuple-element.223.w_in, ...), custom_call_target="tpu_custom_call" | custom-call | flops 4831838208 | bytes 15728640 | tf_op jit(solution)/shard_map/feed/pallas_call | solution.py:899
  219.0 5.2 %second_norm.1 = (f32[512,768]{1,0:T(8,128)}, f32[512,768]{1,0:T(8,128)}, bf16[512,768]{1,0:T(8,128)(2,1)}, f32[8,768]{1,0:T(8,128)}) custom-call(s32[2]{0:T(128)} %subtract_clamp_fusion.1.counts, f32[512,768]{1,0:T(8,128)} %get-tuple-element.221.normal_ref, f32[512,768]{1,0:T(8,128)} %get-tuple-element.226.mine_ref, bf16[512,768]{1,0:T(8,128)(2,1)} %copy-done.10, ...), custom_call_target="tpu_custom_call" | custom-call | flops 7864320 | bytes 9437184 | tf_op jit(solution)/shard_map/second_norm/pallas_call | solution.py:1074
  224.7 2.1 collective-permute-done.39.low_came
  227.7 19.2 %feed_back.1 = (f32[512,768]{1,0:T(8,128)}, bf16[512,768]{1,0:T(8,128)(2,1)}, f32[1,1536]{1,0:T(1,128)}, bf16[384,3072]{1,0:T(8,128)(2,1)}, bf16[384,3072]{1,0:T(8,128)(2,1)}) custom-call(s32[2]{0:T(128)} %pad_add_fusion.1.where, bf16[512,768]{1,0:T(8,128)(2,1)} %get-tuple-element.230.low_own, bf16[512,768]{1,0:T(8,128)(2,1)} %copy-done.60, ...), custom_call_target="tpu_custom_call" | custom-call | flops 9663676416 | bytes 22020096 | tf_op jit(solution)/shard_map/feed_back/pallas_call | solution.py:973
  247.3 2.1 collective-permute-done.40.came_ref
  250.3 4.3 first_norm_back.1
  254.9 2.1 collective-permute-done.41.came_ref
  258.0 4.7 turn.1
  266.4 4.3 output_grad.1
  271.3 4.5 collective-permute-done.42.g_oth
  276.6 50.3 %attend_back.2 = (f32[384,512]{1,0:T(8,128)}, bf16[384,512]{1,0:T(8,128)(2,1)}, bf16[1024,768]{1,0:T(8,128)(2,1)}, bf16[1024,768]{1,0:T(8,128)(2,1)}, f32[1,768]{1,0:T(1,128)}, /*index=5*/f32[768,768]{1,0:T(8,128)}) custom-call(s32[7]{0:T(128)} %get-tuple-element.386.counts, bf16[1024,384]{1,0:T(8,128)(2,1)} %get-tuple-element.237.both, ...), custom_call_target="tpu_custom_call" | custom-call | flops 32212254720 | bytes 22020096 | tf_op jit(solution)/shard_map/attend_back/pallas_call | solution.py:639
  327.8 3.4 collective-permute-start.48
  332.5 3.8 fold_sides.2
  336.3 2.0 collective-permute-start.51
  338.4 2.1 convert_add_fusion.1
  342.7 2.3 collective-permute-start.52
  345.0 19.5 %attend_back.3 = (f32[384,512]{1,0:T(8,128)}, bf16[384,512]{1,0:T(8,128)(2,1)}, bf16[1024,768]{1,0:T(8,128)(2,1)}, bf16[1024,768]{1,0:T(8,128)(2,1)}, f32[1,768]...) custom-call(s32[7]{0:T(128)} %get-tuple-element.387.counts, bf16[1024,384]{1,0:T(8,128)(2,1)} %get-tuple-element.247.both, ...), custom_call_target="tpu_custom_call" | custom-call | flops 32212254720 | bytes 22020096 | tf_op jit(solution)/shard_map/attend_back/pallas_call | solution.py:639
  364.5 3.4 collective-permute-done.51.came_ref
  367.9 8.8 %collective-permute-done.53 = bf16[256,768]{1,0:T(8,128)(2,1)S(1)} collective-permute-done((bf16[256,768]{1,0:T(8,128)(2,1)S(1)}, bf16[256,768]{1,0:T(8,128)(2,1)S(1)}, u32[]{:S(2)}, u32[]{:S(2)}) %collective-permute-start.53) | collective-permute-done | bytes 393248 | tf_op jit(solution)/shard_map/ppermute | solution.py:46
  376.8 2.7 add_low.1
  379.5 3.5 all-to-all-start
  383.4 19.4 %collective-permute-start.59 = (bf16[384,768]{1,0:T(8,128)(2,1)}, bf16[384,768]{1,0:T(8,128)(2,1)S(1)}, u32[]{:S(2)}, u32[]{:S(2)}) collective-permute-start(bf16[384,768]{1,0:T(8,128)(2,1)} %get-tuple-element.287), channel_id=1, source_target_pairs={{0,16},{16,0},{1,17},{17,1},{2,18},{18,2},{3,19},{19,3},{4,20},{20... | collective-permute-start | bytes 1769480 | tf_op jit(solution)/shard_map/ppermute | solution.py:46
  404.0 4.0 fusion.9
  410.3 6.6 %collective-permute-start.61 = (bf16[256,768]{1,0:T(8,128)(2,1)}, bf16[256,768]{1,0:T(8,128)(2,1)}, u32[]{:S(2)}, u32[]{:S(2)}) collective-permute-start(bf16[256,768]{1,0:T(8,128)(2,1)} %get-tuple-element.360), channel_id=1, source_target_pairs={{12,8},{0,4},{13,9},{1,5},{14,10},{2,6},{15,11},{3,7},{28,24},{16,... | collective-permute-start | bytes 1179656 | tf_op jit(solution)/shard_map/ppermute | solution.py:1377
  417.6 6.2 %query_back.1 = (f32[512,768]{1,0:T(8,128)}, bf16[512,768]{1,0:T(8,128)(2,1)}, f32[384,1]{1,0:T(8,128)}, f32[384,384]{1,0:T(8,128)}, bf16[384,384]{1,0:T(8,128)(2,1)}) custom-call(s32[2]{0:T(128)} %pad_add_fusion.1.where, f32[384,512]{1,0:T(8,128)} %get-tuple-element.246.refs_0_, f32[384,512]{1,0:T(8,128)} %get-tuple-element.269.refs_1_, ...), custom_call_target="tpu_custom_call" | custom-call | flops 1207959552 | bytes 8848896 | tf_op jit(solution)/shard_map/query_back/pallas_call | solution.py:68
  425.1 2.0 collective-permute-start.60
  427.1 5.9 %collective-permute-done.60 = f32[1,6912]{1,0:T(1,128)S(1)} collective-permute-done((f32[1,6912]{1,0:T(1,128)S(1)}, f32[1,6912]{1,0:T(1,128)S(1)}, u32[]{:S(2)}, u32[]{:S(2)}) %collective-permute-start.60) | collective-permute-done | bytes 27680 | tf_op jit(solution)/shard_map/ppermute | solution.py:46
  433.1 2.1 add_convert_fusion
  435.2 3.3 fold_sides.3
  438.8 2.0 collective-permute-start.65
  442.8 14.9 %collective-permute-done.66 = bf16[256,768]{1,0:T(8,128)(2,1)} collective-permute-done((bf16[256,768]{1,0:T(8,128)(2,1)}, bf16[256,768]{1,0:T(8,128)(2,1)}, u32[]{:S(2)}, u32[]{:S(2)}) %collective-permute-start.66) | collective-permute-done | bytes 393248 | tf_op jit(solution)/shard_map/ppermute | solution.py:46
  457.7 2.2 collective-permute-done.65
  460.7 2.7 fold_spots.1
  463.4 2.0 collective-permute-start.68
  465.4 2.4 collective-permute-start.69
  468.0 2.2 fusion.3
  472.3 6.9 %collective-permute-done.68 = bf16[112,768]{1,0:T(8,128)(2,1)S(1)} collective-permute-done((bf16[112,768]{1,0:T(8,128)(2,1)}, bf16[112,768]{1,0:T(8,128)(2,1)S(1)}, u32[]{:S(2)}, u32[]{:S(2)}) %collective-permute-start.68) | collective-permute-done | bytes 172064 | tf_op jit(solution)/shard_map/ppermute | solution.py:46
  (317 shorter events, 68.0 us)
Async XLA Ops:
  0.7 19.4 %collective-permute-start = (bf16[2,256,768]{2,1,0:T(8,128)(2,1)}, bf16[2,256,768]{2,1,0:T(8,128)(2,1)S(1)}, u32[]{:S(2)}, u32[]{:S(2)}) collective-permute-start(bf16[2,256,768]{2,1,0:T(8,128)(2,1)} %param.18), channel_id=1, source_target_pairs={{0,1},{1,0},{2,3},{3,2},{4,5},{5,4},{6,7},{7,6},{8,9},{9,8},{10,11... | collective-permute-start | bytes 2359304 | tf_op jit(solution)/shard_map/ppermute | solution.py:46
  1.2 20.9 %collective-permute-start.1 = (bf16[2,256,768]{2,1,0:T(8,128)(2,1)}, bf16[2,256,768]{2,1,0:T(8,128)(2,1)S(1)}, u32[]{:S(2)}, u32[]{:S(2)}) collective-permute-start(bf16[2,256,768]{2,1,0:T(8,128)(2,1)} %param.18), channel_id=1, source_target_pairs={{0,2},{1,3},{2,0},{3,1},{4,6},{5,7},{6,4},{7,5},{8,10},{9,11},{10,... | collective-permute-start | bytes 2359304 | tf_op jit(solution)/shard_map/ppermute | solution.py:46
  5.5 8.3 %collective-permute-start.4 = (bf16[96,640]{1,0:T(8,128)(2,1)}, bf16[96,640]{1,0:T(8,128)(2,1)S(1)}, u32[]{:S(2)}, u32[]{:S(2)}) collective-permute-start(bf16[96,640]{1,0:T(8,128)(2,1)} %pack.2.refs_0_), channel_id=1, source_target_pairs={{0,12},{4,8},{8,4},{12,0},{1,13},{5,9},{9,5},{13,1},{2,14},{6,10},... | collective-permute-start | bytes 368648 | tf_op jit(solution)/shard_map/ppermute | solution.py:46
  9.1 10.9 %collective-permute-start.3 = (bf16[96,640]{1,0:T(8,128)(2,1)}, bf16[96,640]{1,0:T(8,128)(2,1)S(1)}, u32[]{:S(2)}, u32[]{:S(2)}) collective-permute-start(bf16[96,640]{1,0:T(8,128)(2,1)} %pack.2.refs_0_), channel_id=1, source_target_pairs={{0,8},{4,12},{8,0},{12,4},{1,9},{5,13},{9,1},{13,5},{2,10},{6,14},... | collective-permute-start | bytes 368648 | tf_op jit(solution)/shard_map/ppermute | solution.py:46
  9.1 10.9 %collective-permute-start.2 = (bf16[96,640]{1,0:T(8,128)(2,1)}, bf16[96,640]{1,0:T(8,128)(2,1)S(1)}, u32[]{:S(2)}, u32[]{:S(2)}) collective-permute-start(bf16[96,640]{1,0:T(8,128)(2,1)} %pack.2.refs_0_), channel_id=1, source_target_pairs={{0,4},{4,0},{8,12},{12,8},{1,5},{5,1},{9,13},{13,9},{2,6},{6,2},{1... | collective-permute-start | bytes 368648 | tf_op jit(solution)/shard_map/ppermute | solution.py:46
  24.1 24.5 %collective-permute-start.7 = (bf16[384,640]{1,0:T(8,128)(2,1)}, bf16[384,640]{1,0:T(8,128)(2,1)S(1)}, u32[]{:S(2)}, u32[]{:S(2)}) collective-permute-start(bf16[384,640]{1,0:T(8,128)(2,1)} %stack.98.refs_0_), channel_id=1, source_target_pairs={{0,18},{1,19},{2,16},{3,17},{16,2},{17,3},{18,0},{19,1},{4,22},{5,... | collective-permute-start | bytes 1474568 | tf_op jit(solution)/shard_map/ppermute | solution.py:1181
  26.7 22.1 %collective-permute-start.6 = (bf16[384,640]{1,0:T(8,128)(2,1)}, bf16[384,640]{1,0:T(8,128)(2,1)S(1)}, u32[]{:S(2)}, u32[]{:S(2)}) collective-permute-start(bf16[384,640]{1,0:T(8,128)(2,1)} %stack.98.refs_0_), channel_id=1, source_target_pairs={{0,16},{16,0},{1,17},{17,1},{2,18},{18,2},{3,19},{19,3},{4,20},{20... | collective-permute-start | bytes 1474568 | tf_op jit(solution)/shard_map/ppermute | solution.py:46
  27.3 21.6 %collective-permute-start.5 = (bf16[384,640]{1,0:T(8,128)(2,1)}, bf16[384,640]{1,0:T(8,128)(2,1)}, u32[]{:S(2)}, u32[]{:S(2)}) collective-permute-start(bf16[384,640]{1,0:T(8,128)(2,1)} %stack.98.refs_0_), channel_id=1, source_target_pairs={{0,2},{1,3},{2,0},{3,1},{4,6},{5,7},{6,4},{7,5},{8,10},{9,11},{10,... | collective-permute-start | bytes 1474568 | tf_op jit(solution)/shard_map/ppermute | solution.py:46
  27.7 18.5 %collective-permute-start.9 = (bf16[256,768]{1,0:T(8,128)(2,1)S(1)}, bf16[256,768]{1,0:T(8,128)(2,1)}, u32[]{:S(2)}, u32[]{:S(2)}) collective-permute-start(bf16[256,768]{1,0:T(8,128)(2,1)S(1)} %get-tuple-element.176.refs_0_.refs_4_), channel_id=1, source_target_pairs={{0,4},{4,0},{8,12},{12,8},{1,5},{5,1},{9,13},{13,9},{2,6},{6,2},{1... | collective-permute-start | bytes 1179656 | tf_op jit(solution)/shard_map/ppermute | solution.py:46
  29.5 19.0 %collective-permute-start.8 = (bf16[256,768]{1,0:T(8,128)(2,1)S(1)}, bf16[256,768]{1,0:T(8,128)(2,1)}, u32[]{:S(2)}, u32[]{:S(2)}) collective-permute-start(bf16[256,768]{1,0:T(8,128)(2,1)S(1)} %get-tuple-element.176.refs_0_.refs_4_), channel_id=1, source_target_pairs={{0,8},{4,12},{8,0},{12,4},{1,9},{5,13},{9,1},{13,5},{2,10},{6,14},... | collective-permute-start | bytes 1179656 | tf_op jit(solution)/shard_map/ppermute | solution.py:46
  48.8 14.6 %collective-permute-start.14 = (bf16[256,768]{1,0:T(8,128)(2,1)}, bf16[256,768]{1,0:T(8,128)(2,1)}, u32[]{:S(2)}, u32[]{:S(2)}) collective-permute-start(bf16[256,768]{1,0:T(8,128)(2,1)} %collective-permute-done.9.refs_2_), channel_id=1, source_target_pairs={{0,1},{1,0},{2,3},{3,2},{4,5},{5,4},{6,7},{7,6},{8,9},{9,8},{10,11... | collective-permute-start | bytes 1179656 | tf_op jit(solution)/shard_map/ppermute | solution.py:46
  48.8 14.6 %collective-permute-start.13 = (bf16[256,768]{1,0:T(8,128)(2,1)}, bf16[256,768]{1,0:T(8,128)(2,1)}, u32[]{:S(2)}, u32[]{:S(2)}) collective-permute-start(bf16[256,768]{1,0:T(8,128)(2,1)} %collective-permute-done.8.refs_4_), channel_id=1, source_target_pairs={{0,1},{1,0},{2,3},{3,2},{4,5},{5,4},{6,7},{7,6},{8,9},{9,8},{10,11... | collective-permute-start | bytes 1179656 | tf_op jit(solution)/shard_map/ppermute | solution.py:46
  49.3 14.1 %collective-permute-start.12 = (bf16[256,768]{1,0:T(8,128)(2,1)}, bf16[256,768]{1,0:T(8,128)(2,1)}, u32[]{:S(2)}, u32[]{:S(2)}) collective-permute-start(bf16[256,768]{1,0:T(8,128)(2,1)} %collective-permute-done.8.refs_4_), channel_id=1, source_target_pairs={{8,12},{4,0},{9,13},{5,1},{10,14},{6,2},{11,15},{7,3},{24,28},{20,... | collective-permute-start | bytes 1179656 | tf_op jit(solution)/shard_map/ppermute | solution.py:1168
  50.6 12.8 %collective-permute-start.11 = (bf16[256,768]{1,0:T(8,128)(2,1)S(1)}, bf16[256,768]{1,0:T(8,128)(2,1)}, u32[]{:S(2)}, u32[]{:S(2)}) collective-permute-start(bf16[256,768]{1,0:T(8,128)(2,1)S(1)} %get-tuple-element.176.refs_0_.refs_4_), channel_id=1, source_target_pairs={{4,8},{8,4},{5,9},{9,5},{6,10},{10,6},{7,11},{11,7},{20,24},{24,20... | collective-permute-start | bytes 1179656 | tf_op jit(solution)/shard_map/ppermute | solution.py:1167
  53.0 10.3 %collective-permute-start.10 = (f32[1,1152]{1,0:T(1,128)S(1)}, f32[1,1152]{1,0:T(1,128)S(1)}, u32[]{:S(2)}, u32[]{:S(2)}) collective-permute-start(f32[1,1152]{1,0:T(1,128)S(1)} %broadcast_in_dim.12), channel_id=1, source_target_pairs={{0,2},{1,3},{2,0},{3,1},{4,6},{5,7},{6,4},{7,5},{8,10},{9,11},{10,... | collective-permute-start | bytes 13832 | tf_op jit(solution)/shard_map/ppermute | solution.py:46
  63.4 10.2 %collective-permute-start.16 = (bf16[256,768]{1,0:T(8,128)(2,1)S(1)}, bf16[256,768]{1,0:T(8,128)(2,1)S(1)}, u32[]{:S(2)}, u32[]{:S(2)}) collective-permute-start(bf16[256,768]{1,0:T(8,128)(2,1)S(1)} %get-tuple-element.366.refs_8_), channel_id=1, source_target_pairs={{0,1},{1,0},{2,3},{3,2},{4,5},{5,4},{6,7},{7,6},{8,9},{9,8},{10,11... | collective-permute-start | bytes 1179656 | tf_op jit(solution)/shard_map/ppermute | solution.py:46
  64.5 40.8 %collective-permute-start.19 = (bf16[96,1792]{1,0:T(8,128)(2,1)S(1)}, bf16[96,1792]{1,0:T(8,128)(2,1)S(1)}, u32[]{:S(2)}, u32[]{:S(2)}) collective-permute-start(bf16[96,1792]{1,0:T(8,128)(2,1)S(1)} %copy-done.8), channel_id=1, source_target_pairs={{0,12},{4,8},{8,4},{12,0},{1,13},{5,9},{9,5},{13,1},{2,14},{6,10},... | collective-permute-start | bytes 1032200 | tf_op jit(solution)/shard_map/ppermute | solution.py:46
  68.2 37.2 %collective-permute-start.18 = (bf16[96,1792]{1,0:T(8,128)(2,1)S(1)}, bf16[96,1792]{1,0:T(8,128)(2,1)S(1)}, u32[]{:S(2)}, u32[]{:S(2)}) collective-permute-start(bf16[96,1792]{1,0:T(8,128)(2,1)S(1)} %copy-done.8), channel_id=1, source_target_pairs={{0,8},{4,12},{8,0},{12,4},{1,9},{5,13},{9,1},{13,5},{2,10},{6,14},... | collective-permute-start | bytes 1032200 | tf_op jit(solution)/shard_map/ppermute | solution.py:46
  72.6 32.8 %collective-permute-start.17 = (bf16[96,1792]{1,0:T(8,128)(2,1)S(1)}, bf16[96,1792]{1,0:T(8,128)(2,1)S(1)}, u32[]{:S(2)}, u32[]{:S(2)}) collective-permute-start(bf16[96,1792]{1,0:T(8,128)(2,1)S(1)} %copy-done.8), channel_id=1, source_target_pairs={{0,4},{4,0},{8,12},{12,8},{1,5},{5,1},{9,13},{13,9},{2,6},{6,2},{1... | collective-permute-start | bytes 1032200 | tf_op jit(solution)/shard_map/ppermute | solution.py:46
  72.6 3.0 collective-permute-start.15
  73.5 36.2 %collective-permute-start.21 = (bf16[256,768]{1,0:T(8,128)(2,1)S(1)}, bf16[256,768]{1,0:T(8,128)(2,1)S(1)}, u32[]{:S(2)}, u32[]{:S(2)}) collective-permute-start(bf16[256,768]{1,0:T(8,128)(2,1)S(1)} %get-tuple-element.198.refs_0_.refs_5_), channel_id=1, source_target_pairs={{0,4},{4,0},{8,12},{12,8},{1,5},{5,1},{9,13},{13,9},{2,6},{6,2},{1... | collective-permute-start | bytes 1179656 | tf_op jit(solution)/shard_map/ppermute | solution.py:46
  75.6 40.3 %collective-permute-start.20 = (bf16[256,768]{1,0:T(8,128)(2,1)S(1)}, bf16[256,768]{1,0:T(8,128)(2,1)S(1)}, u32[]{:S(2)}, u32[]{:S(2)}) collective-permute-start(bf16[256,768]{1,0:T(8,128)(2,1)S(1)} %get-tuple-element.198.refs_0_.refs_5_), channel_id=1, source_target_pairs={{0,8},{4,12},{8,0},{12,4},{1,9},{5,13},{9,1},{13,5},{2,10},{6,14},... | collective-permute-start | bytes 1179656 | tf_op jit(solution)/shard_map/ppermute | solution.py:46
  105.4 11.0 %collective-permute-start.24 = (bf16[256,768]{1,0:T(8,128)(2,1)S(1)}, bf16[256,768]{1,0:T(8,128)(2,1)S(1)}, u32[]{:S(2)}, u32[]{:S(2)}) collective-permute-start(bf16[256,768]{1,0:T(8,128)(2,1)S(1)} %get-tuple-element.198.refs_0_.refs_5_), channel_id=1, source_target_pairs={{4,8},{8,4},{5,9},{9,5},{6,10},{10,6},{7,11},{11,7},{20,24},{24,20... | collective-permute-start | bytes 1179656 | tf_op jit(solution)/shard_map/ppermute | solution.py:1167
  108.9 26.9 %collective-permute-start.22 = (bf16[384,1024]{1,0:T(8,128)(2,1)}, bf16[384,1024]{1,0:T(8,128)(2,1)S(1)}, u32[]{:S(2)}, u32[]{:S(2)}) collective-permute-start(bf16[384,1024]{1,0:T(8,128)(2,1)} %get-tuple-element.212.refs_0_), channel_id=1, source_target_pairs={{0,2},{1,3},{2,0},{3,1},{4,6},{5,7},{6,4},{7,5},{8,10},{9,11},{10,... | collective-permute-start | bytes 2359304 | tf_op jit(solution)/shard_map/ppermute | solution.py:46
  108.9 26.9 %collective-permute-start.23 = (bf16[384,768]{1,0:T(8,128)(2,1)}, bf16[384,768]{1,0:T(8,128)(2,1)S(1)}, u32[]{:S(2)}, u32[]{:S(2)}) collective-permute-start(bf16[384,768]{1,0:T(8,128)(2,1)} %get-tuple-element.214.refs_0_), channel_id=1, source_target_pairs={{0,16},{16,0},{1,17},{17,1},{2,18},{18,2},{3,19},{19,3},{4,20},{20... | collective-permute-start | bytes 1769480 | tf_op jit(solution)/shard_map/ppermute | solution.py:46
  116.5 19.2 %collective-permute-start.25 = (bf16[256,768]{1,0:T(8,128)(2,1)S(1)}, bf16[256,768]{1,0:T(8,128)(2,1)S(1)}, u32[]{:S(2)}, u32[]{:S(2)}) collective-permute-start(bf16[256,768]{1,0:T(8,128)(2,1)S(1)} %collective-permute-done.20.refs_4_), channel_id=1, source_target_pairs={{8,12},{4,0},{9,13},{5,1},{10,14},{6,2},{11,15},{7,3},{24,28},{20,... | collective-permute-start | bytes 1179656 | tf_op jit(solution)/shard_map/ppermute | solution.py:1168
  118.0 20.5 %collective-permute-start.29 = (bf16[256,768]{1,0:T(8,128)(2,1)}, bf16[256,768]{1,0:T(8,128)(2,1)}, u32[]{:S(2)}, u32[]{:S(2)}) collective-permute-start(bf16[256,768]{1,0:T(8,128)(2,1)} %get-tuple-element.365.refs_8_), channel_id=1, source_target_pairs={{0,1},{1,0},{2,3},{3,2},{4,5},{5,4},{6,7},{7,6},{8,9},{9,8},{10,11... | collective-permute-start | bytes 1179656 | tf_op jit(solution)/shard_map/ppermute | solution.py:46
  135.8 4.1 collective-permute-start.28
  135.9 44.6 %collective-permute-start.30 = (bf16[432,512]{1,0:T(8,128)(2,1)S(1)}, bf16[432,512]{1,0:T(8,128)(2,1)S(1)}, u32[]{:S(2)}, u32[]{:S(2)}) collective-permute-start(bf16[432,512]{1,0:T(8,128)(2,1)S(1)} %copy-done.61), channel_id=1, source_target_pairs={{0,2},{1,3},{2,0},{3,1},{4,6},{5,7},{6,4},{7,5},{8,10},{9,11},{10,... | collective-permute-start | bytes 1327112 | tf_op jit(solution)/shard_map/ppermute | solution.py:46
  136.4 25.2 %collective-permute-start.34 = (bf16[384,768]{1,0:T(8,128)(2,1)}, bf16[384,768]{1,0:T(8,128)(2,1)S(1)}, u32[]{:S(2)}, u32[]{:S(2)}) collective-permute-start(bf16[384,768]{1,0:T(8,128)(2,1)} %get-tuple-element.214.refs_0_), channel_id=1, source_target_pairs={{0,2},{1,3},{2,0},{3,1},{4,6},{5,7},{6,4},{7,5},{8,10},{9,11},{10,... | collective-permute-start | bytes 1769480 | tf_op jit(solution)/shard_map/ppermute | solution.py:46
  138.0 36.2 %collective-permute-start.35 = (bf16[384,768]{1,0:T(8,128)(2,1)S(1)}, bf16[384,768]{1,0:T(8,128)(2,1)S(1)}, u32[]{:S(2)}, u32[]{:S(2)}) collective-permute-start(bf16[384,768]{1,0:T(8,128)(2,1)S(1)} %collective-permute-done.23.refs_2_), channel_id=1, source_target_pairs={{0,2},{1,3},{2,0},{3,1},{4,6},{5,7},{6,4},{7,5},{8,10},{9,11},{10,... | collective-permute-start | bytes 1769480 | tf_op jit(solution)/shard_map/ppermute | solution.py:46
  138.5 35.8 %collective-permute-start.32 = (bf16[384,1024]{1,0:T(8,128)(2,1)}, bf16[384,1024]{1,0:T(8,128)(2,1)S(1)}, u32[]{:S(2)}, u32[]{:S(2)}) collective-permute-start(bf16[384,1024]{1,0:T(8,128)(2,1)} %get-tuple-element.212.refs_0_), channel_id=1, source_target_pairs={{0,16},{16,0},{1,17},{17,1},{2,18},{18,2},{3,19},{19,3},{4,20},{20... | collective-permute-start | bytes 2359304 | tf_op jit(solution)/shard_map/ppermute | solution.py:46
  139.9 34.6 %collective-permute-start.33 = (bf16[384,1024]{1,0:T(8,128)(2,1)S(1)}, bf16[384,1024]{1,0:T(8,128)(2,1)S(1)}, u32[]{:S(2)}, u32[]{:S(2)}) collective-permute-start(bf16[384,1024]{1,0:T(8,128)(2,1)S(1)} %collective-permute-done.22.refs_1_), channel_id=1, source_target_pairs={{0,16},{16,0},{1,17},{17,1},{2,18},{18,2},{3,19},{19,3},{4,20},{20... | collective-permute-start | bytes 2359304 | tf_op jit(solution)/shard_map/ppermute | solution.py:46
  161.6 21.7 %collective-permute-start.31 = (bf16[432,512]{1,0:T(8,128)(2,1)}, bf16[432,512]{1,0:T(8,128)(2,1)S(1)}, u32[]{:S(2)}, u32[]{:S(2)}) collective-permute-start(bf16[432,512]{1,0:T(8,128)(2,1)} %get-tuple-element.210), channel_id=1, source_target_pairs={{0,2},{1,3},{2,0},{3,1},{4,6},{5,7},{6,4},{7,5},{8,10},{9,11},{10,... | collective-permute-start | bytes 1327112 | tf_op jit(solution)/shard_map/ppermute | solution.py:46
  195.9 4.6 collective-permute-start.37
  262.6 13.2 %collective-permute-start.42 = (bf16[432,512]{1,0:T(8,128)(2,1)}, bf16[432,512]{1,0:T(8,128)(2,1)S(1)}, u32[]{:S(2)}, u32[]{:S(2)}) collective-permute-start(bf16[432,512]{1,0:T(8,128)(2,1)} %get-tuple-element.241.g_own), channel_id=1, source_target_pairs={{0,2},{1,3},{2,0},{3,1},{4,6},{5,7},{6,4},{7,5},{8,10},{9,11},{10,... | collective-permute-start | bytes 1327112 | tf_op jit(solution)/shard_map/ppermute | solution.py:46
  263.1 68.1 %collective-permute-start.49 = (bf16[384,3072]{1,0:T(8,128)(2,1)S(1)}, bf16[384,3072]{1,0:T(8,128)(2,1)S(1)}, u32[]{:S(2)}, u32[]{:S(2)}) collective-permute-start(bf16[384,3072]{1,0:T(8,128)(2,1)S(1)} %copy-done.58), channel_id=1, source_target_pairs={{0,16},{16,0},{1,17},{17,1},{2,18},{18,2},{3,19},{19,3},{4,20},{20... | collective-permute-start | bytes 7077896 | tf_op jit(solution)/shard_map/ppermute | solution.py:46
  264.7 6.6 %collective-permute-start.43 = (f32[6,768]{1,0:T(8,128)S(1)}, f32[6,768]{1,0:T(8,128)S(1)}, u32[]{:S(2)}, u32[]{:S(2)}) collective-permute-start(f32[6,768]{1,0:T(8,128)S(1)} %pad_maximum_fusion.1), channel_id=1, source_target_pairs={{0,1},{1,0},{2,3},{3,2},{4,5},{5,4},{6,7},{7,6},{8,9},{9,8},{10,11... | collective-permute-start | bytes 55304 | tf_op jit(solution)/shard_map/ppermute | solution.py:46
  264.7 62.1 %collective-permute-start.44 = (bf16[432,512]{1,0:T(8,128)(2,1)}, bf16[432,512]{1,0:T(8,128)(2,1)S(1)}, u32[]{:S(2)}, u32[]{:S(2)}) collective-permute-start(bf16[432,512]{1,0:T(8,128)(2,1)} %get-tuple-element.248.g_own), channel_id=1, source_target_pairs={{0,2},{1,3},{2,0},{3,1},{4,6},{5,7},{6,4},{7,5},{8,10},{9,11},{10,... | collective-permute-start | bytes 1327112 | tf_op jit(solution)/shard_map/ppermute | solution.py:46
  270.7 56.1 %collective-permute-start.45 = (bf16[384,384]{1,0:T(8,128)(2,1)}, bf16[384,384]{1,0:T(8,128)(2,1)S(1)}, u32[]{:S(2)}, u32[]{:S(2)}) collective-permute-start(bf16[384,384]{1,0:T(8,128)(2,1)} %get-tuple-element.253), channel_id=1, source_target_pairs={{0,16},{16,0},{1,17},{17,1},{2,18},{18,2},{3,19},{19,3},{4,20},{20... | collective-permute-start | bytes 884744 | tf_op jit(solution)/shard_map/ppermute | solution.py:46
  275.9 51.0 %collective-permute-start.46 = (f32[1,6144]{1,0:T(1,128)S(1)}, f32[1,6144]{1,0:T(1,128)S(1)}, u32[]{:S(2)}, u32[]{:S(2)}) collective-permute-start(f32[1,6144]{1,0:T(1,128)S(1)} %constant_dynamic-update-slice_fusion.6), channel_id=1, source_target_pairs={{0,4},{4,0},{8,12},{12,8},{1,5},{5,1},{9,13},{13,9},{2,6},{6,2},{1... | collective-permute-start | bytes 73736 | tf_op jit(solution)/shard_map/ppermute | solution.py:46
  327.7 10.6 %collective-permute-start.50 = (bf16[1024,768]{1,0:T(8,128)(2,1)}, bf16[1024,768]{1,0:T(8,128)(2,1)S(1)}, u32[]{:S(2)}, u32[]{:S(2)}) collective-permute-start(bf16[1024,768]{1,0:T(8,128)(2,1)} %get-tuple-element.265), channel_id=1, source_target_pairs={{0,1},{1,0},{2,3},{3,2},{4,5},{5,4},{6,7},{7,6},{8,9},{9,8},{10,11... | collective-permute-start | bytes 4718600 | tf_op jit(solution)/shard_map/ppermute | solution.py:46
  327.8 14.9 %collective-permute-start.48 = (f32[1,6144]{1,0:T(1,128)S(1)}, f32[1,6144]{1,0:T(1,128)S(1)}, u32[]{:S(2)}, u32[]{:S(2)}) collective-permute-start(f32[1,6144]{1,0:T(1,128)S(1)} %add.120), channel_id=1, source_target_pairs={{0,8},{4,12},{8,0},{12,4},{1,9},{5,13},{9,1},{13,5},{2,10},{6,14},... | collective-permute-start | bytes 73736 | tf_op jit(solution)/shard_map/ppermute | solution.py:46
  331.1 13.8 %collective-permute-start.47 = (bf16[384,512]{1,0:T(8,128)(2,1)}, bf16[384,512]{1,0:T(8,128)(2,1)S(1)}, u32[]{:S(2)}, u32[]{:S(2)}) collective-permute-start(bf16[384,512]{1,0:T(8,128)(2,1)} %get-tuple-element.257), channel_id=1, source_target_pairs={{0,2},{1,3},{2,0},{3,1},{4,6},{5,7},{6,4},{7,5},{8,10},{9,11},{10,... | collective-permute-start | bytes 1179656 | tf_op jit(solution)/shard_map/ppermute | solution.py:46
  336.3 31.5 %collective-permute-start.51 = (bf16[384,1536]{1,0:T(8,128)(2,1)}, bf16[384,1536]{1,0:T(8,128)(2,1)S(1)}, u32[]{:S(2)}, u32[]{:S(2)}) collective-permute-start(bf16[384,1536]{1,0:T(8,128)(2,1)} %get-tuple-element.263), channel_id=1, source_target_pairs={{0,2},{1,3},{2,0},{3,1},{4,6},{5,7},{6,4},{7,5},{8,10},{9,11},{10,... | collective-permute-start | bytes 3538952 | tf_op jit(solution)/shard_map/ppermute | solution.py:46
  340.5 27.4 %collective-permute-start.54 = (bf16[256,768]{1,0:T(8,128)(2,1)S(1)}, bf16[256,768]{1,0:T(8,128)(2,1)S(1)}, u32[]{:S(2)}, u32[]{:S(2)}) collective-permute-start(bf16[256,768]{1,0:T(8,128)(2,1)S(1)} %get-tuple-element.362), channel_id=1, source_target_pairs={{0,12},{4,8},{8,4},{12,0},{1,13},{5,9},{9,5},{13,1},{2,14},{6,10},... | collective-permute-start | bytes 1179656 | tf_op jit(solution)/shard_map/ppermute | solution.py:46
  341.0 35.6 %collective-permute-start.53 = (bf16[256,768]{1,0:T(8,128)(2,1)S(1)}, bf16[256,768]{1,0:T(8,128)(2,1)S(1)}, u32[]{:S(2)}, u32[]{:S(2)}) collective-permute-start(bf16[256,768]{1,0:T(8,128)(2,1)S(1)} %get-tuple-element.363), channel_id=1, source_target_pairs={{0,8},{4,12},{8,0},{12,4},{1,9},{5,13},{9,1},{13,5},{2,10},{6,14},... | collective-permute-start | bytes 1179656 | tf_op jit(solution)/shard_map/ppermute | solution.py:46
  342.7 33.9 %collective-permute-start.52 = (bf16[256,768]{1,0:T(8,128)(2,1)S(1)}, bf16[256,768]{1,0:T(8,128)(2,1)S(1)}, u32[]{:S(2)}, u32[]{:S(2)}) collective-permute-start(bf16[256,768]{1,0:T(8,128)(2,1)S(1)} %get-tuple-element.364), channel_id=1, source_target_pairs={{0,4},{4,0},{8,12},{12,8},{1,5},{5,1},{9,13},{13,9},{2,6},{6,2},{1... | collective-permute-start | bytes 1179656 | tf_op jit(solution)/shard_map/ppermute | solution.py:46
  376.6 26.2 %collective-permute-start.56 = (bf16[1024,768]{1,0:T(8,128)(2,1)}, bf16[1024,768]{1,0:T(8,128)(2,1)S(1)}, u32[]{:S(2)}, u32[]{:S(2)}) collective-permute-start(bf16[1024,768]{1,0:T(8,128)(2,1)} %get-tuple-element.279), channel_id=1, source_target_pairs={{0,1},{1,0},{2,3},{3,2},{4,5},{5,4},{6,7},{7,6},{8,9},{9,8},{10,11... | collective-permute-start | bytes 4718600 | tf_op jit(solution)/shard_map/ppermute | solution.py:46
  379.5 63.2 %all-to-all-start = ((bf16[4,96,1536]{2,1,0:T(8,128)(2,1)}), bf16[4,96,1536]{2,1,0:T(8,128)(2,1)S(1)}, u32[]{:S(2)}, u32[]{:S(2)}) async-start(bf16[4,96,1536]{2,1,0:T(8,128)(2,1)} %bitcast.48), calls=%async_computation | async-start | bytes 2359296 | tf_op jit(solution)/shard_map/all_to_all | solution.py:1362
  383.0 33.8 %collective-permute-start.55 = (bf16[384,512]{1,0:T(8,128)(2,1)}, bf16[384,512]{1,0:T(8,128)(2,1)S(1)}, u32[]{:S(2)}, u32[]{:S(2)}) collective-permute-start(bf16[384,512]{1,0:T(8,128)(2,1)} %get-tuple-element.275), channel_id=1, source_target_pairs={{0,2},{1,3},{2,0},{3,1},{4,6},{5,7},{6,4},{7,5},{8,10},{9,11},{10,... | collective-permute-start | bytes 1179656 | tf_op jit(solution)/shard_map/ppermute | solution.py:46
  383.4 49.6 %collective-permute-start.59 = (bf16[384,768]{1,0:T(8,128)(2,1)}, bf16[384,768]{1,0:T(8,128)(2,1)S(1)}, u32[]{:S(2)}, u32[]{:S(2)}) collective-permute-start(bf16[384,768]{1,0:T(8,128)(2,1)} %get-tuple-element.287), channel_id=1, source_target_pairs={{0,16},{16,0},{1,17},{17,1},{2,18},{18,2},{3,19},{19,3},{4,20},{20... | collective-permute-start | bytes 1769480 | tf_op jit(solution)/shard_map/ppermute | solution.py:46
  408.9 24.1 %collective-permute-start.62 = (bf16[256,768]{1,0:T(8,128)(2,1)}, bf16[256,768]{1,0:T(8,128)(2,1)}, u32[]{:S(2)}, u32[]{:S(2)}) collective-permute-start(bf16[256,768]{1,0:T(8,128)(2,1)} %get-tuple-element.360), channel_id=1, source_target_pairs={{4,8},{8,4},{5,9},{9,5},{6,10},{10,6},{7,11},{11,7},{20,24},{24,20... | collective-permute-start | bytes 1179656 | tf_op jit(solution)/shard_map/ppermute | solution.py:1378
  410.3 22.7 %collective-permute-start.61 = (bf16[256,768]{1,0:T(8,128)(2,1)}, bf16[256,768]{1,0:T(8,128)(2,1)}, u32[]{:S(2)}, u32[]{:S(2)}) collective-permute-start(bf16[256,768]{1,0:T(8,128)(2,1)} %get-tuple-element.360), channel_id=1, source_target_pairs={{12,8},{0,4},{13,9},{1,5},{14,10},{2,6},{15,11},{3,7},{28,24},{16,... | collective-permute-start | bytes 1179656 | tf_op jit(solution)/shard_map/ppermute | solution.py:1377
  425.0 8.0 %collective-permute-start.58 = (bf16[384,384]{1,0:T(8,128)(2,1)}, bf16[384,384]{1,0:T(8,128)(2,1)S(1)}, u32[]{:S(2)}, u32[]{:S(2)}) collective-permute-start(bf16[384,384]{1,0:T(8,128)(2,1)} %get-tuple-element.286), channel_id=1, source_target_pairs={{0,16},{16,0},{1,17},{17,1},{2,18},{18,2},{3,19},{19,3},{4,20},{20... | collective-permute-start | bytes 884744 | tf_op jit(solution)/shard_map/ppermute | solution.py:46
  425.1 7.9 %collective-permute-start.60 = (f32[1,6912]{1,0:T(1,128)S(1)}, f32[1,6912]{1,0:T(1,128)S(1)}, u32[]{:S(2)}, u32[]{:S(2)}) collective-permute-start(f32[1,6912]{1,0:T(1,128)S(1)} %constant_dynamic-update-slice_fusion.8), channel_id=1, source_target_pairs={{0,16},{16,0},{1,17},{17,1},{2,18},{18,2},{3,19},{19,3},{4,20},{20... | collective-permute-start | bytes 82952 | tf_op jit(solution)/shard_map/ppermute | solution.py:46
  433.0 9.6 %collective-permute-start.57 = (bf16[512,768]{1,0:T(8,128)(2,1)}, bf16[512,768]{1,0:T(8,128)(2,1)S(1)}, u32[]{:S(2)}, u32[]{:S(2)}) collective-permute-start(bf16[512,768]{1,0:T(8,128)(2,1)} %get-tuple-element.282), channel_id=1, source_target_pairs={{0,1},{1,0},{2,3},{3,2},{4,5},{5,4},{6,7},{7,6},{8,9},{9,8},{10,11... | collective-permute-start | bytes 2359304 | tf_op jit(solution)/shard_map/ppermute | solution.py:46
  438.5 21.4 %collective-permute-start.63 = (bf16[384,768]{1,0:T(8,128)(2,1)}, bf16[384,768]{1,0:T(8,128)(2,1)S(1)}, u32[]{:S(2)}, u32[]{:S(2)}) collective-permute-start(bf16[384,768]{1,0:T(8,128)(2,1)} %get-tuple-element.301), channel_id=1, source_target_pairs={{0,2},{1,3},{2,0},{3,1},{4,6},{5,7},{6,4},{7,5},{8,10},{9,11},{10,... | collective-permute-start | bytes 1769480 | tf_op jit(solution)/shard_map/ppermute | solution.py:46
  438.8 18.9 %collective-permute-start.66 = (bf16[256,768]{1,0:T(8,128)(2,1)}, bf16[256,768]{1,0:T(8,128)(2,1)}, u32[]{:S(2)}, u32[]{:S(2)}) collective-permute-start(bf16[256,768]{1,0:T(8,128)(2,1)} %get-tuple-element.361), channel_id=1, source_target_pairs={{0,4},{4,0},{8,12},{12,8},{1,5},{5,1},{9,13},{13,9},{2,6},{6,2},{1... | collective-permute-start | bytes 1179656 | tf_op jit(solution)/shard_map/ppermute | solution.py:46
  438.8 21.1 %collective-permute-start.65 = (bf16[256,768]{1,0:T(8,128)(2,1)}, bf16[256,768]{1,0:T(8,128)(2,1)}, u32[]{:S(2)}, u32[]{:S(2)}) collective-permute-start(bf16[256,768]{1,0:T(8,128)(2,1)} %add_convert_fusion), channel_id=1, source_target_pairs={{0,8},{4,12},{8,0},{12,4},{1,9},{5,13},{9,1},{13,5},{2,10},{6,14},... | collective-permute-start | bytes 1179656 | tf_op jit(solution)/shard_map/ppermute | solution.py:46
  440.8 16.8 %collective-permute-start.64 = (f32[1,6912]{1,0:T(1,128)S(1)}, f32[1,6912]{1,0:T(1,128)S(1)}, u32[]{:S(2)}, u32[]{:S(2)}) collective-permute-start(f32[1,6912]{1,0:T(1,128)S(1)} %add.132), channel_id=1, source_target_pairs={{0,2},{1,3},{2,0},{3,1},{4,6},{5,7},{6,4},{7,5},{8,10},{9,11},{10,... | collective-permute-start | bytes 82952 | tf_op jit(solution)/shard_map/ppermute | solution.py:46
  463.4 8.9 %collective-permute-start.67 = (bf16[112,768]{1,0:T(8,128)(2,1)}, bf16[112,768]{1,0:T(8,128)(2,1)S(1)}, u32[]{:S(2)}, u32[]{:S(2)}) collective-permute-start(bf16[112,768]{1,0:T(8,128)(2,1)} %get-tuple-element.309), channel_id=1, source_target_pairs={{0,4},{4,0},{8,12},{12,8},{1,5},{5,1},{9,13},{13,9},{2,6},{6,2},{1... | collective-permute-start | bytes 516104 | tf_op jit(solution)/shard_map/ppermute | solution.py:46
  463.4 15.8 %collective-permute-start.68 = (bf16[112,768]{1,0:T(8,128)(2,1)}, bf16[112,768]{1,0:T(8,128)(2,1)S(1)}, u32[]{:S(2)}, u32[]{:S(2)}) collective-permute-start(bf16[112,768]{1,0:T(8,128)(2,1)} %get-tuple-element.310), channel_id=1, source_target_pairs={{0,8},{4,12},{8,0},{12,4},{1,9},{5,13},{9,1},{13,5},{2,10},{6,14},... | collective-permute-start | bytes 516104 | tf_op jit(solution)/shard_map/ppermute | solution.py:46
  465.4 13.8 %collective-permute-start.69 = (bf16[112,768]{1,0:T(8,128)(2,1)}, bf16[112,768]{1,0:T(8,128)(2,1)S(1)}, u32[]{:S(2)}, u32[]{:S(2)}) collective-permute-start(bf16[112,768]{1,0:T(8,128)(2,1)} %get-tuple-element.311), channel_id=1, source_target_pairs={{0,12},{4,8},{8,4},{12,0},{1,13},{5,9},{9,5},{13,1},{2,14},{6,10},... | collective-permute-start | bytes 516104 | tf_op jit(solution)/shard_map/ppermute | solution.py:46
  (80 other events, 739.9 us)
where the time goes:
time: 485 us; the launch traced here: 482 us
  Pallas kernels  212 us (44%)
  waiting for transfers between devices  129 us (27%)
  starting transfers between devices  97.4 us (20%)
  local copies, waits for them, and re-layouts  23.5 us (5%)
  other arithmetic  18.9 us (4%)
    ppermute x63, waiting for transfers between devices, swap(): lax.ppermute(after(value, *start), axis, [(i, i ^ bit) for i in range(cou...  111 us
    ppermute x63, starting transfers between devices, swap(): lax.ppermute(after(value, *start), axis, [(i, i ^ bit) for i in range(cou...  78.2 us
    pallas_call x2, Pallas kernels, attend_back(): pl.pallas_call(functools.partial(attend_back_kernel, slots, pairs, split,...  69.8 us
    pallas_call x2, Pallas kernels, attend(): pl.pallas_call(functools.partial(attend_kernel, slots, min(128, keys), le...  42.5 us
    pallas_call x9, Pallas kernels, call(): pl.pallas_call(kernel, grid_spec=pltpu.PrefetchScalarGridSpec(num_scalar_...  29.7 us
    pallas_call x1, Pallas kernels, feed_back(): pl.pallas_call(functools.partial(feed_back_kernel, half, lines), grid_spe...  19.2 us
    ppermute x2, waiting for transfers between devices, send_last(): lax.ppermute(far, 'ctx', [(2, 3), (1, 0)])  17.5 us
    pallas_call x1, Pallas kernels, feed(): pl.pallas_call(functools.partial(feed_kernel, units // 3 if units % 384 =...  14.2 us
  transfers between devices with their start and end apart: 71, of which 25 were waited for; matrix products, arithmetic and copies ran while one was open for 5% of the time, Pallas kernels for 31%

commit v1 on v0

--- a/solution.py
+++ b/solution.py
@@ -226,19 +226,19 @@
     count = vector.shape[0]
     below_rows = 3 * count + -3 * count % 16
     if not fits(rows):
-        total = kept + came.astype(F32)
+        total = kept.astype(F32) + came.astype(F32)
         cut = lambda k: lax.dynamic_slice_in_dim(total, (spot ^ k) * rows, rows, 0)
         terms = jnp.concatenate([*in_three(vector), jnp.zeros((below_rows - 3 * count, width), BF)], axis=0)
         return [cut(0)] + [jnp.concatenate([cut(k).astype(BF), terms], axis=0) for k in range(1, spots)]
 
     def kernel(where, kept_ref, came_ref, vector_ref, own, *outs):
         at = pl.ds(pl.multiple_of(where[0] * rows, rows), rows)
-        own[...] = kept_ref[at, :] + came_ref[at, :].astype(F32)
+        own[...] = kept_ref[at, :].astype(F32) + came_ref[at, :].astype(F32)
         terms = jnp.concatenate(in_three(vector_ref[...]), axis=0)
         terms = jnp.concatenate([terms, jnp.zeros((below_rows - 3 * count, width), BF)], axis=0)
         for k, out in enumerate(outs):
             at = pl.ds(pl.multiple_of((where[0] ^ (k + 1)) * rows, rows), rows)
-            out[:rows, :] = (kept_ref[at, :] + came_ref[at, :].astype(F32)).astype(BF)
+            out[:rows, :] = (kept_ref[at, :].astype(F32) + came_ref[at, :].astype(F32)).astype(BF)
             out[rows:, :] = terms
 
     outs = [((rows, width), F32)] + [((rows + below_rows, width), BF)] * (spots - 1)
@@ -294,7 +294,7 @@
         )
         part = dot(low, weight[...], (((0,), (1,)), ((), ())))
         to = slice(s * half, s * half + half)
-        mine_ref[to, :] = jnp.where(upper, part[half:], part[:half])
+        mine_ref[to, :] = jnp.where(upper, part[half:], part[:half]).astype(BF)
         other_ref[to, :] = jnp.where(upper, part[:half], part[half:]).astype(BF)
         grad = dot(rows, low, (((0,), (1,)), ((), ())))
         total[...] = grad if s == 0 else total[...] + grad
@@ -313,7 +313,7 @@
     seqs, lines = len(dq_own), lax.axis_size("dp")
     local, width = own[0].shape
     own_width = weight.shape[1]
-    outs = [((seqs * local, width), F32), ((seqs * local, width), BF), ((own_width, 1), F32)]
+    outs = [((seqs * local, width), BF), ((seqs * local, width), BF), ((own_width, 1), F32)]
     if lines == 2:
         outs += [((width // 2, own_width), F32), ((width // 2, own_width), BF)]
     else:
@@ -1365,7 +1365,7 @@
     mine, other, query_bias_sum, *query_grads = query_back(
         where, dq_own, dq_came, x_rows, [came[s] for s in range(seqs)], query_full
     )
-    query_term = (mine + other_core(other).astype(F32)).reshape(seqs, local, width)
+    query_term = (mine.astype(F32) + other_core(other).astype(F32)).reshape(seqs, local, width)
     query_pair = over_lines(query_grads)
     value_bias_sum = apart(kv_bias_sum)[1]
     vector = jnp.concatenate([early, query_bias_sum.reshape(1, -1), value_bias_sum], axis=1)
@@ -1404,6 +1404,7 @@
     kept, sent = fold_sides(
         [query_pair, kv_pair, output_pair],
         [sides_of(0, heads_width), side_cuts(1, 0), side_cuts(1, PAIR), sides_of(2, heads_width)],
+        BF,
     )
     vector_came = other_side(vector)
     term, feed_spread, vector_came, *rest = together(other_side(sent), feed_spread, vector_came, *came_1[1:])

time: 485 us -> 482 us (level)
  Pallas kernels: 212 us -> 179 us
  waiting for transfers between devices: 129 us -> 157 us
    ppermute x63, waiting for transfers between devices: 111 us -> 140 us  [swap(): lax.ppermute(after(value, *start), axis, [(i, i ^ bit) for i in range(cou...]
    pallas_call x2, Pallas kernels: 69.8 us -> 48.1 us  [attend_back(): pl.pallas_call(functools.partial(attend_back_kernel, slots, pairs, split,...]
    pallas_call x2, Pallas kernels: 42.5 us -> 32 us  [attend(): pl.pallas_call(functools.partial(attend_kernel, slots, min(128, keys), le...]
    unnamed x156 -> x162, local copies, waits for them, and re-layouts: 13.8 us -> 13.6 us
  transfers between devices with their start and end apart: 71 -> 71, of which waited for: 25 -> 26; matrix products, arithmetic and copies ran while one was open for 5% -> 6% of each run, Pallas kernels for 31% -> 25%
where the time goes in v1:
time: 482 us; the launch traced here: 476 us
  Pallas kernels  179 us (37%)
  waiting for transfers between devices  157 us (33%)
  starting transfers between devices  95.7 us (20%)
  local copies, waits for them, and re-layouts  23.4 us (5%)
  other arithmetic  19 us (4%)
    ppermute x63, waiting for transfers between devices, swap(): lax.ppermute(after(value, *start), axis, [(i, i ^ bit) for i in range(cou...  140 us
    ppermute x63, starting transfers between devices, swap(): lax.ppermute(after(value, *start), axis, [(i, i ^ bit) for i in range(cou...  76.6 us
    pallas_call x2, Pallas kernels, attend_back(): pl.pallas_call(functools.partial(attend_back_kernel, slots, pairs, split,...  48.1 us
    pallas_call x2, Pallas kernels, attend(): pl.pallas_call(functools.partial(attend_kernel, slots, min(128, keys), le...  32 us
    pallas_call x9, Pallas kernels, call(): pl.pallas_call(kernel, grid_spec=pltpu.PrefetchScalarGridSpec(num_scalar_...  29 us
    pallas_call x1, Pallas kernels, feed_back(): pl.pallas_call(functools.partial(feed_back_kernel, half, lines), grid_spe...  19.2 us
    ppermute x2, waiting for transfers between devices, send_last(): lax.ppermute(far, 'ctx', [(2, 3), (1, 0)])  17.3 us
    pallas_call x1, Pallas kernels, feed(): pl.pallas_call(functools.partial(feed_kernel, units // 3 if units % 384 =...  14.3 us
  transfers between devices with their start and end apart: 71, of which 26 were waited for; matrix products, arithmetic and copies ran while one was open for 6% of the time, Pallas kernels for 25%

profile of v1, /device:TPU:0, one launch (start us, length us, event | category | flops | bytes accessed | tf_op | source)
XLA Modules:
  0.0 475.9 jit_solution(7403917420992662156)
XLA Ops:
  1.2 2.6 collective-permute-start.1
  5.5 3.6 collective-permute-start.4
  13.8 6.2 %collective-permute-done.3.refs_2_ = bf16[96,640]{1,0:T(8,128)(2,1)S(1)} collective-permute-done((bf16[96,640]{1,0:T(8,128)(2,1)}, bf16[96,640]{1,0:T(8,128)(2,1)S(1)}, u32[]{:S(2)}, u32[]{:S(2)}) %collective-permute-start.3) | collective-permute-done | bytes 122912 | tf_op jit(solution)/shard_map/ppermute | solution.py:46
  20.1 2.1 collective-permute-done.1
  24.1 2.7 collective-permute-start.7
  30.1 2.6 collective-permute-start.8
  33.3 13.4 %collective-permute-done.9.refs_2_ = bf16[256,768]{1,0:T(8,128)(2,1)} collective-permute-done((bf16[256,768]{1,0:T(8,128)(2,1)S(1)}, bf16[256,768]{1,0:T(8,128)(2,1)}, u32[]{:S(2)}, u32[]{:S(2)}) %collective-permute-start.9) | collective-permute-done | bytes 393248 | tf_op jit(solution)/shard_map/ppermute | solution.py:46
  46.7 2.4 collective-permute-done.8.refs_4_
  55.7 2.0 copy.39.refs_2_
  57.7 2.1 pack.3.refs_0_
  59.8 3.9 place.3
  64.9 3.3 collective-permute-start.19
  68.2 4.4 collective-permute-start.18
  73.6 2.1 collective-permute-start.21
  76.4 18.5 %attend.2 = (bf16[1024,384]{1,0:T(8,128)(2,1)}, bf16[2048,768]{1,0:T(8,128)(2,1)}, f32[2,384,512]{2,1,0:T(8,128)}, bf16[432,512]{1,0:T(8,128)(2,1)}, f32[2,3,2,512]{3,2,1,0:T(2,128)}) custom-call(s32[7]{0:T(128)} %get-tuple-element.386.counts, bf16[256,768]{1,0:T(8,128)(2,1)} %copy-done.2, bf16[256,768]{1,0:T(8,128)(2,1)} %get-tuple-element.367.refs_1_.refs_6_, ...), custom_call_target="tpu_custom_call" | custom-call | flops 12884901888 | bytes 10223616 | tf_op jit(solution)/shard_map/attend/pallas_call | solution.py:483
  94.9 4.6 collective-permute-done.18.refs_2_
  100.3 2.5 stack.99
  104.8 11.5 %collective-permute-done.20.refs_4_ = bf16[256,768]{1,0:T(8,128)(2,1)S(1)} collective-permute-done((bf16[256,768]{1,0:T(8,128)(2,1)S(1)}, bf16[256,768]{1,0:T(8,128)(2,1)S(1)}, u32[]{:S(2)}, u32[]{:S(2)}) %collective-permute-start.20) | collective-permute-done | bytes 393248 | tf_op jit(solution)/shard_map/ppermute | solution.py:46
  118.6 17.3 %collective-permute-done.25 = bf16[256,768]{1,0:T(8,128)(2,1)S(1)} collective-permute-done((bf16[256,768]{1,0:T(8,128)(2,1)S(1)}, bf16[256,768]{1,0:T(8,128)(2,1)S(1)}, u32[]{:S(2)}, u32[]{:S(2)}) %collective-permute-start.25) | collective-permute-done | bytes 393248 | tf_op jit(solution)/shard_map/ppermute | solution.py:1168
  140.9 13.6 %attend.3 = (bf16[1024,384]{1,0:T(8,128)(2,1)}, bf16[2048,768]{1,0:T(8,128)(2,1)}, f32[2,384,512]{2,1,0:T(8,128)}, bf16[432,512]{1,0:T(8,128)(2,1)}, f32[2,3,2,512]{3,2,1,0:T(2,128)}) custom-call(s32[7]{0:T(128)} %get-tuple-element.387.counts, bf16[256,768]{1,0:T(8,128)(2,1)} %copy-done.3, ...), custom_call_target="tpu_custom_call", output_to_operand_aliasing={{2}: (15, {}), {4}: (16, {})} | custom-call | flops 12884901888 | bytes 10223616 | tf_op jit(solution)/shard_map/attend/pallas_call | solution.py:483
  154.5 7.2 %collective-permute-done.34.refs_1_ = bf16[384,768]{1,0:T(8,128)(2,1)S(1)} collective-permute-done((bf16[384,768]{1,0:T(8,128)(2,1)}, bf16[384,768]{1,0:T(8,128)(2,1)S(1)}, u32[]{:S(2)}, u32[]{:S(2)}) %collective-permute-start.34) | collective-permute-done | bytes 589856 | tf_op jit(solution)/shard_map/ppermute | solution.py:46
  162.8 11.5 %collective-permute-done.35.refs_3_ = bf16[384,768]{1,0:T(8,128)(2,1)S(1)} collective-permute-done((bf16[384,768]{1,0:T(8,128)(2,1)S(1)}, bf16[384,768]{1,0:T(8,128)(2,1)S(1)}, u32[]{:S(2)}, u32[]{:S(2)}) %collective-permute-start.35) | collective-permute-done | bytes 589856 | tf_op jit(solution)/shard_map/ppermute | solution.py:46
  175.7 4.9 %place.4 = (bf16[768,384]{1,0:T(8,128)(2,1)}, bf16[768,1536]{1,0:T(8,128)(2,1)}) custom-call(s32[3]{0:T(128)} %get-tuple-element.389.where, bf16[384,1024]{1,0:T(8,128)(2,1)} %get-tuple-element.212.refs_0_, bf16[384,1024]{1,0:T(8,128)(2,1)} %copy-done.12, bf16[384,1024]{1,0:T(8,128)(2,1)} %copy-done.13, bf16[384,1024]{1,0:T(8,128)(2,1)} %copy-done.14), custom_call_target="tpu_custom_call" | custom-call | bytes 9043968 | tf_op jit(solution)/shard_map/place/pallas_call | solution.py:68
  180.7 2.7 collective-permute-done.31.refs_1_
  184.1 5.1 %merge.1 = (f32[2,384,512]{2,1,0:T(8,128)}, bf16[2,384,512]{2,1,0:T(8,128)(2,1)}, f32[2,256,768]{2,1,0:T(8,128)}, bf16[2,256,768]{2,1,0:T(8,128)(2,1)}, f32[2,3,2,512]{3,2,1,0:T(2,128)}) custom-call(s32[2]{0:T(128)} %pad_add_fusion.1.where, f32[2,384,512]{2,1,0:T(8,128)} %get-tuple-element.205.o_own, f32[2,3,2,512]{3,2,1,0:T(2,128)} %get-tuple-element.206.lse_own, ...), custom_call_target="tpu_custom_call" | custom-call | flops 603979776 | bytes 7864320 | tf_op jit(solution)/shard_map/merge/pallas_call | solution.py:725
  192.6 3.4 first_norm.1
  196.8 3.9 place.5.w_out
  201.6 14.3 %feed.1 = (bf16[1024,1536]{1,0:T(8,128)(2,1)}, bf16[1024,1536]{1,0:T(8,128)(2,1)}, f32[512,768]{1,0:T(8,128)}, bf16[512,768]{1,0:T(8,128)(2,1)}) custom-call(bf16[512,768]{1,0:T(8,128)(2,1)} %get-tuple-element.222.own_ref, bf16[512,768]{1,0:T(8,128)(2,1)} %copy-done.61, bf16[768,1536]{1,0:T(8,128)(2,1)} %get-tuple-element.223.w_in, ...), custom_call_target="tpu_custom_call" | custom-call | flops 4831838208 | bytes 15728640 | tf_op jit(solution)/shard_map/feed/pallas_call | solution.py:899
  219.2 5.2 %second_norm.1 = (f32[512,768]{1,0:T(8,128)}, f32[512,768]{1,0:T(8,128)}, bf16[512,768]{1,0:T(8,128)(2,1)}, f32[8,768]{1,0:T(8,128)}) custom-call(s32[2]{0:T(128)} %subtract_clamp_fusion.1.counts, f32[512,768]{1,0:T(8,128)} %get-tuple-element.221.normal_ref, f32[512,768]{1,0:T(8,128)} %get-tuple-element.226.mine_ref, bf16[512,768]{1,0:T(8,128)(2,1)} %copy-done.9, ...), custom_call_target="tpu_custom_call" | custom-call | flops 7864320 | bytes 9437184 | tf_op jit(solution)/shard_map/second_norm/pallas_call | solution.py:1074
  224.9 2.1 collective-permute-done.39.low_came
  227.9 19.2 %feed_back.1 = (f32[512,768]{1,0:T(8,128)}, bf16[512,768]{1,0:T(8,128)(2,1)}, f32[1,1536]{1,0:T(1,128)}, bf16[384,3072]{1,0:T(8,128)(2,1)}, bf16[384,3072]{1,0:T(8,128)(2,1)}) custom-call(s32[2]{0:T(128)} %pad_add_fusion.1.where, bf16[512,768]{1,0:T(8,128)(2,1)} %get-tuple-element.230.low_own, bf16[512,768]{1,0:T(8,128)(2,1)} %copy-done.62, ...), custom_call_target="tpu_custom_call" | custom-call | flops 9663676416 | bytes 22020096 | tf_op jit(solution)/shard_map/feed_back/pallas_call | solution.py:973
  247.5 2.1 collective-permute-done.40.came_ref
  250.5 4.3 first_norm_back.1
  255.2 2.1 collective-permute-done.41.came_ref
  258.2 4.6 turn.1
  266.6 4.3 output_grad.1
  271.5 4.5 collective-permute-done.42.g_oth
  276.8 28.6 %attend_back.2 = (f32[384,512]{1,0:T(8,128)}, bf16[384,512]{1,0:T(8,128)(2,1)}, bf16[1024,768]{1,0:T(8,128)(2,1)}, bf16[1024,768]{1,0:T(8,128)(2,1)}, f32[1,768]{1,0:T(1,128)}, /*index=5*/f32[768,768]{1,0:T(8,128)}) custom-call(s32[7]{0:T(128)} %get-tuple-element.386.counts, bf16[1024,384]{1,0:T(8,128)(2,1)} %get-tuple-element.237.both, ...), custom_call_target="tpu_custom_call" | custom-call | flops 32212254720 | bytes 22020096 | tf_op jit(solution)/shard_map/attend_back/pallas_call | solution.py:639
  305.5 17.5 %collective-permute-done.45.refs_5_ = bf16[384,384]{1,0:T(8,128)(2,1)S(1)} collective-permute-done((bf16[384,384]{1,0:T(8,128)(2,1)}, bf16[384,384]{1,0:T(8,128)(2,1)S(1)}, u32[]{:S(2)}, u32[]{:S(2)}) %collective-permute-start.45) | collective-permute-done | bytes 294944 | tf_op jit(solution)/shard_map/ppermute | solution.py:46
  327.5 3.8 fold_sides.2
  331.7 2.1 convert_add_fusion.1
  333.9 2.1 collective-permute-start.54
  336.0 1.9 collective-permute-start.53
  338.4 19.5 %attend_back.3 = (f32[384,512]{1,0:T(8,128)}, bf16[384,512]{1,0:T(8,128)(2,1)}, bf16[1024,768]{1,0:T(8,128)(2,1)}, bf16[1024,768]{1,0:T(8,128)(2,1)}, f32[1,768]...) custom-call(s32[7]{0:T(128)} %get-tuple-element.387.counts, bf16[1024,384]{1,0:T(8,128)(2,1)} %get-tuple-element.247.both, ...), custom_call_target="tpu_custom_call" | custom-call | flops 32212254720 | bytes 22020096 | tf_op jit(solution)/shard_map/attend_back/pallas_call | solution.py:639
  357.9 3.3 collective-permute-done.51.came_ref
  361.2 10.5 %collective-permute-done.53 = bf16[256,768]{1,0:T(8,128)(2,1)S(1)} collective-permute-done((bf16[256,768]{1,0:T(8,128)(2,1)S(1)}, bf16[256,768]{1,0:T(8,128)(2,1)S(1)}, u32[]{:S(2)}, u32[]{:S(2)}) %collective-permute-start.53) | collective-permute-done | bytes 393248 | tf_op jit(solution)/shard_map/ppermute | solution.py:46
  371.8 2.7 add_low.1
  374.6 3.5 all-to-all-start
  379.8 17.5 %collective-permute-start.59 = (bf16[384,768]{1,0:T(8,128)(2,1)}, bf16[384,768]{1,0:T(8,128)(2,1)S(1)}, u32[]{:S(2)}, u32[]{:S(2)}) collective-permute-start(bf16[384,768]{1,0:T(8,128)(2,1)} %get-tuple-element.287), channel_id=1, source_target_pairs={{0,16},{16,0},{1,17},{17,1},{2,18},{18,2},{3,19},{19,3},{4,20},{20... | collective-permute-start | bytes 1769480 | tf_op jit(solution)/shard_map/ppermute | solution.py:46
  398.5 4.0 fusion.9
  404.8 6.6 %collective-permute-start.61 = (bf16[256,768]{1,0:T(8,128)(2,1)}, bf16[256,768]{1,0:T(8,128)(2,1)}, u32[]{:S(2)}, u32[]{:S(2)}) collective-permute-start(bf16[256,768]{1,0:T(8,128)(2,1)} %get-tuple-element.360), channel_id=1, source_target_pairs={{12,8},{0,4},{13,9},{1,5},{14,10},{2,6},{15,11},{3,7},{28,24},{16,... | collective-permute-start | bytes 1179656 | tf_op jit(solution)/shard_map/ppermute | solution.py:1377
  412.2 6.0 %query_back.1 = (bf16[512,768]{1,0:T(8,128)(2,1)}, bf16[512,768]{1,0:T(8,128)(2,1)}, f32[384,1]{1,0:T(8,128)}, f32[384,384]{1,0:T(8,128)}, bf16[384,384]{1,0:T(8,128)(2,1)}) custom-call(s32[2]{0:T(128)} %pad_add_fusion.1.where, f32[384,512]{1,0:T(8,128)} %get-tuple-element.246.refs_0_, f32[384,512]{1,0:T(8,128)} %get-tuple-element.269.refs_1_, ...), custom_call_target="tpu_custom_call" | custom-call | flops 1207959552 | bytes 8848896 | tf_op jit(solution)/shard_map/query_back/pallas_call | solution.py:68
  419.4 2.0 collective-permute-start.60
  421.4 5.9 %collective-permute-done.60 = f32[1,6912]{1,0:T(1,128)S(1)} collective-permute-done((f32[1,6912]{1,0:T(1,128)S(1)}, f32[1,6912]{1,0:T(1,128)S(1)}, u32[]{:S(2)}, u32[]{:S(2)}) %collective-permute-start.60) | collective-permute-done | bytes 27680 | tf_op jit(solution)/shard_map/ppermute | solution.py:46
  427.3 2.1 add_convert_fusion
  429.5 3.1 fold_sides.3
  433.1 2.0 collective-permute-start.65
  436.9 15.0 %collective-permute-done.66 = bf16[256,768]{1,0:T(8,128)(2,1)} collective-permute-done((bf16[256,768]{1,0:T(8,128)(2,1)}, bf16[256,768]{1,0:T(8,128)(2,1)}, u32[]{:S(2)}, u32[]{:S(2)}) %collective-permute-start.66) | collective-permute-done | bytes 393248 | tf_op jit(solution)/shard_map/ppermute | solution.py:46
  451.9 2.1 collective-permute-done.65
  454.8 2.2 fold_spots.1
  457.0 2.0 collective-permute-start.68
  459.1 2.4 collective-permute-start.69
  461.6 2.2 fusion.3
  465.9 6.9 %collective-permute-done.68 = bf16[112,768]{1,0:T(8,128)(2,1)S(1)} collective-permute-done((bf16[112,768]{1,0:T(8,128)(2,1)}, bf16[112,768]{1,0:T(8,128)(2,1)S(1)}, u32[]{:S(2)}, u32[]{:S(2)}) %collective-permute-start.68) | collective-permute-done | bytes 172064 | tf_op jit(solution)/shard_map/ppermute | solution.py:46
  (323 shorter events, 73.7 us)
Async XLA Ops:
  0.7 19.4 %collective-permute-start = (bf16[2,256,768]{2,1,0:T(8,128)(2,1)}, bf16[2,256,768]{2,1,0:T(8,128)(2,1)S(1)}, u32[]{:S(2)}, u32[]{:S(2)}) collective-permute-start(bf16[2,256,768]{2,1,0:T(8,128)(2,1)} %param.18), channel_id=1, source_target_pairs={{0,1},{1,0},{2,3},{3,2},{4,5},{5,4},{6,7},{7,6},{8,9},{9,8},{10,11... | collective-permute-start | bytes 2359304 | tf_op jit(solution)/shard_map/ppermute | solution.py:46
  1.2 20.9 %collective-permute-start.1 = (bf16[2,256,768]{2,1,0:T(8,128)(2,1)}, bf16[2,256,768]{2,1,0:T(8,128)(2,1)S(1)}, u32[]{:S(2)}, u32[]{:S(2)}) collective-permute-start(bf16[2,256,768]{2,1,0:T(8,128)(2,1)} %param.18), channel_id=1, source_target_pairs={{0,2},{1,3},{2,0},{3,1},{4,6},{5,7},{6,4},{7,5},{8,10},{9,11},{10,... | collective-permute-start | bytes 2359304 | tf_op jit(solution)/shard_map/ppermute | solution.py:46
  5.5 8.3 %collective-permute-start.4 = (bf16[96,640]{1,0:T(8,128)(2,1)}, bf16[96,640]{1,0:T(8,128)(2,1)S(1)}, u32[]{:S(2)}, u32[]{:S(2)}) collective-permute-start(bf16[96,640]{1,0:T(8,128)(2,1)} %pack.2.refs_0_), channel_id=1, source_target_pairs={{0,12},{4,8},{8,4},{12,0},{1,13},{5,9},{9,5},{13,1},{2,14},{6,10},... | collective-permute-start | bytes 368648 | tf_op jit(solution)/shard_map/ppermute | solution.py:46
  9.1 10.9 %collective-permute-start.3 = (bf16[96,640]{1,0:T(8,128)(2,1)}, bf16[96,640]{1,0:T(8,128)(2,1)S(1)}, u32[]{:S(2)}, u32[]{:S(2)}) collective-permute-start(bf16[96,640]{1,0:T(8,128)(2,1)} %pack.2.refs_0_), channel_id=1, source_target_pairs={{0,8},{4,12},{8,0},{12,4},{1,9},{5,13},{9,1},{13,5},{2,10},{6,14},... | collective-permute-start | bytes 368648 | tf_op jit(solution)/shard_map/ppermute | solution.py:46
  9.1 10.9 %collective-permute-start.2 = (bf16[96,640]{1,0:T(8,128)(2,1)}, bf16[96,640]{1,0:T(8,128)(2,1)S(1)}, u32[]{:S(2)}, u32[]{:S(2)}) collective-permute-start(bf16[96,640]{1,0:T(8,128)(2,1)} %pack.2.refs_0_), channel_id=1, source_target_pairs={{0,4},{4,0},{8,12},{12,8},{1,5},{5,1},{9,13},{13,9},{2,6},{6,2},{1... | collective-permute-start | bytes 368648 | tf_op jit(solution)/shard_map/ppermute | solution.py:46
  24.1 25.0 %collective-permute-start.7 = (bf16[384,640]{1,0:T(8,128)(2,1)}, bf16[384,640]{1,0:T(8,128)(2,1)S(1)}, u32[]{:S(2)}, u32[]{:S(2)}) collective-permute-start(bf16[384,640]{1,0:T(8,128)(2,1)} %stack.98.refs_0_), channel_id=1, source_target_pairs={{0,18},{1,19},{2,16},{3,17},{16,2},{17,3},{18,0},{19,1},{4,22},{5,... | collective-permute-start | bytes 1474568 | tf_op jit(solution)/shard_map/ppermute | solution.py:1181
  26.7 22.4 %collective-permute-start.6 = (bf16[384,640]{1,0:T(8,128)(2,1)}, bf16[384,640]{1,0:T(8,128)(2,1)S(1)}, u32[]{:S(2)}, u32[]{:S(2)}) collective-permute-start(bf16[384,640]{1,0:T(8,128)(2,1)} %stack.98.refs_0_), channel_id=1, source_target_pairs={{0,16},{16,0},{1,17},{17,1},{2,18},{18,2},{3,19},{19,3},{4,20},{20... | collective-permute-start | bytes 1474568 | tf_op jit(solution)/shard_map/ppermute | solution.py:46
  27.3 21.8 %collective-permute-start.5 = (bf16[384,640]{1,0:T(8,128)(2,1)}, bf16[384,640]{1,0:T(8,128)(2,1)}, u32[]{:S(2)}, u32[]{:S(2)}) collective-permute-start(bf16[384,640]{1,0:T(8,128)(2,1)} %stack.98.refs_0_), channel_id=1, source_target_pairs={{0,2},{1,3},{2,0},{3,1},{4,6},{5,7},{6,4},{7,5},{8,10},{9,11},{10,... | collective-permute-start | bytes 1474568 | tf_op jit(solution)/shard_map/ppermute | solution.py:46
  28.2 18.5 %collective-permute-start.9 = (bf16[256,768]{1,0:T(8,128)(2,1)S(1)}, bf16[256,768]{1,0:T(8,128)(2,1)}, u32[]{:S(2)}, u32[]{:S(2)}) collective-permute-start(bf16[256,768]{1,0:T(8,128)(2,1)S(1)} %get-tuple-element.176.refs_0_.refs_4_), channel_id=1, source_target_pairs={{0,4},{4,0},{8,12},{12,8},{1,5},{5,1},{9,13},{13,9},{2,6},{6,2},{1... | collective-permute-start | bytes 1179656 | tf_op jit(solution)/shard_map/ppermute | solution.py:46
  30.1 19.0 %collective-permute-start.8 = (bf16[256,768]{1,0:T(8,128)(2,1)S(1)}, bf16[256,768]{1,0:T(8,128)(2,1)}, u32[]{:S(2)}, u32[]{:S(2)}) collective-permute-start(bf16[256,768]{1,0:T(8,128)(2,1)S(1)} %get-tuple-element.176.refs_0_.refs_4_), channel_id=1, source_target_pairs={{0,8},{4,12},{8,0},{12,4},{1,9},{5,13},{9,1},{13,5},{2,10},{6,14},... | collective-permute-start | bytes 1179656 | tf_op jit(solution)/shard_map/ppermute | solution.py:46
  49.1 14.7 %collective-permute-start.14 = (bf16[256,768]{1,0:T(8,128)(2,1)}, bf16[256,768]{1,0:T(8,128)(2,1)}, u32[]{:S(2)}, u32[]{:S(2)}) collective-permute-start(bf16[256,768]{1,0:T(8,128)(2,1)} %collective-permute-done.9.refs_2_), channel_id=1, source_target_pairs={{0,1},{1,0},{2,3},{3,2},{4,5},{5,4},{6,7},{7,6},{8,9},{9,8},{10,11... | collective-permute-start | bytes 1179656 | tf_op jit(solution)/shard_map/ppermute | solution.py:46
  49.2 14.6 %collective-permute-start.13 = (bf16[256,768]{1,0:T(8,128)(2,1)}, bf16[256,768]{1,0:T(8,128)(2,1)}, u32[]{:S(2)}, u32[]{:S(2)}) collective-permute-start(bf16[256,768]{1,0:T(8,128)(2,1)} %collective-permute-done.8.refs_4_), channel_id=1, source_target_pairs={{0,1},{1,0},{2,3},{3,2},{4,5},{5,4},{6,7},{7,6},{8,9},{9,8},{10,11... | collective-permute-start | bytes 1179656 | tf_op jit(solution)/shard_map/ppermute | solution.py:46
  49.7 14.1 %collective-permute-start.12 = (bf16[256,768]{1,0:T(8,128)(2,1)}, bf16[256,768]{1,0:T(8,128)(2,1)}, u32[]{:S(2)}, u32[]{:S(2)}) collective-permute-start(bf16[256,768]{1,0:T(8,128)(2,1)} %collective-permute-done.8.refs_4_), channel_id=1, source_target_pairs={{8,12},{4,0},{9,13},{5,1},{10,14},{6,2},{11,15},{7,3},{24,28},{20,... | collective-permute-start | bytes 1179656 | tf_op jit(solution)/shard_map/ppermute | solution.py:1168
  51.0 12.8 %collective-permute-start.11 = (bf16[256,768]{1,0:T(8,128)(2,1)S(1)}, bf16[256,768]{1,0:T(8,128)(2,1)}, u32[]{:S(2)}, u32[]{:S(2)}) collective-permute-start(bf16[256,768]{1,0:T(8,128)(2,1)S(1)} %get-tuple-element.176.refs_0_.refs_4_), channel_id=1, source_target_pairs={{4,8},{8,4},{5,9},{9,5},{6,10},{10,6},{7,11},{11,7},{20,24},{24,20... | collective-permute-start | bytes 1179656 | tf_op jit(solution)/shard_map/ppermute | solution.py:1167
  53.4 10.4 %collective-permute-start.10 = (f32[1,1152]{1,0:T(1,128)S(1)}, f32[1,1152]{1,0:T(1,128)S(1)}, u32[]{:S(2)}, u32[]{:S(2)}) collective-permute-start(f32[1,1152]{1,0:T(1,128)S(1)} %broadcast_in_dim.12), channel_id=1, source_target_pairs={{0,2},{1,3},{2,0},{3,1},{4,6},{5,7},{6,4},{7,5},{8,10},{9,11},{10,... | collective-permute-start | bytes 13832 | tf_op jit(solution)/shard_map/ppermute | solution.py:46
  63.7 9.8 %collective-permute-start.16 = (bf16[256,768]{1,0:T(8,128)(2,1)S(1)}, bf16[256,768]{1,0:T(8,128)(2,1)S(1)}, u32[]{:S(2)}, u32[]{:S(2)}) collective-permute-start(bf16[256,768]{1,0:T(8,128)(2,1)S(1)} %get-tuple-element.366.refs_8_), channel_id=1, source_target_pairs={{0,1},{1,0},{2,3},{3,2},{4,5},{5,4},{6,7},{7,6},{8,9},{9,8},{10,11... | collective-permute-start | bytes 1179656 | tf_op jit(solution)/shard_map/ppermute | solution.py:46
  64.9 30.0 %collective-permute-start.19 = (bf16[96,1792]{1,0:T(8,128)(2,1)S(1)}, bf16[96,1792]{1,0:T(8,128)(2,1)S(1)}, u32[]{:S(2)}, u32[]{:S(2)}) collective-permute-start(bf16[96,1792]{1,0:T(8,128)(2,1)S(1)} %copy-done.7), channel_id=1, source_target_pairs={{0,12},{4,8},{8,4},{12,0},{1,13},{5,9},{9,5},{13,1},{2,14},{6,10},... | collective-permute-start | bytes 1032200 | tf_op jit(solution)/shard_map/ppermute | solution.py:46
  68.2 31.3 %collective-permute-start.18 = (bf16[96,1792]{1,0:T(8,128)(2,1)S(1)}, bf16[96,1792]{1,0:T(8,128)(2,1)S(1)}, u32[]{:S(2)}, u32[]{:S(2)}) collective-permute-start(bf16[96,1792]{1,0:T(8,128)(2,1)S(1)} %copy-done.7), channel_id=1, source_target_pairs={{0,8},{4,12},{8,0},{12,4},{1,9},{5,13},{9,1},{13,5},{2,10},{6,14},... | collective-permute-start | bytes 1032200 | tf_op jit(solution)/shard_map/ppermute | solution.py:46
  72.6 26.8 %collective-permute-start.17 = (bf16[96,1792]{1,0:T(8,128)(2,1)S(1)}, bf16[96,1792]{1,0:T(8,128)(2,1)S(1)}, u32[]{:S(2)}, u32[]{:S(2)}) collective-permute-start(bf16[96,1792]{1,0:T(8,128)(2,1)S(1)} %copy-done.7), channel_id=1, source_target_pairs={{0,4},{4,0},{8,12},{12,8},{1,5},{5,1},{9,13},{13,9},{2,6},{6,2},{1... | collective-permute-start | bytes 1032200 | tf_op jit(solution)/shard_map/ppermute | solution.py:46
  72.6 3.0 collective-permute-start.15
  73.6 31.2 %collective-permute-start.21 = (bf16[256,768]{1,0:T(8,128)(2,1)S(1)}, bf16[256,768]{1,0:T(8,128)(2,1)S(1)}, u32[]{:S(2)}, u32[]{:S(2)}) collective-permute-start(bf16[256,768]{1,0:T(8,128)(2,1)S(1)} %get-tuple-element.198.refs_0_.refs_5_), channel_id=1, source_target_pairs={{0,4},{4,0},{8,12},{12,8},{1,5},{5,1},{9,13},{13,9},{2,6},{6,2},{1... | collective-permute-start | bytes 1179656 | tf_op jit(solution)/shard_map/ppermute | solution.py:46
  75.6 40.6 %collective-permute-start.20 = (bf16[256,768]{1,0:T(8,128)(2,1)S(1)}, bf16[256,768]{1,0:T(8,128)(2,1)S(1)}, u32[]{:S(2)}, u32[]{:S(2)}) collective-permute-start(bf16[256,768]{1,0:T(8,128)(2,1)S(1)} %get-tuple-element.198.refs_0_.refs_5_), channel_id=1, source_target_pairs={{0,8},{4,12},{8,0},{12,4},{1,9},{5,13},{9,1},{13,5},{2,10},{6,14},... | collective-permute-start | bytes 1179656 | tf_op jit(solution)/shard_map/ppermute | solution.py:46
  99.5 17.3 %collective-permute-start.24 = (bf16[256,768]{1,0:T(8,128)(2,1)S(1)}, bf16[256,768]{1,0:T(8,128)(2,1)S(1)}, u32[]{:S(2)}, u32[]{:S(2)}) collective-permute-start(bf16[256,768]{1,0:T(8,128)(2,1)S(1)} %get-tuple-element.198.refs_0_.refs_5_), channel_id=1, source_target_pairs={{4,8},{8,4},{5,9},{9,5},{6,10},{10,6},{7,11},{11,7},{20,24},{24,20... | collective-permute-start | bytes 1179656 | tf_op jit(solution)/shard_map/ppermute | solution.py:1167
  102.8 33.1 %collective-permute-start.22 = (bf16[384,1024]{1,0:T(8,128)(2,1)}, bf16[384,1024]{1,0:T(8,128)(2,1)S(1)}, u32[]{:S(2)}, u32[]{:S(2)}) collective-permute-start(bf16[384,1024]{1,0:T(8,128)(2,1)} %get-tuple-element.212.refs_0_), channel_id=1, source_target_pairs={{0,2},{1,3},{2,0},{3,1},{4,6},{5,7},{6,4},{7,5},{8,10},{9,11},{10,... | collective-permute-start | bytes 2359304 | tf_op jit(solution)/shard_map/ppermute | solution.py:46
  103.3 32.5 %collective-permute-start.23 = (bf16[384,768]{1,0:T(8,128)(2,1)}, bf16[384,768]{1,0:T(8,128)(2,1)S(1)}, u32[]{:S(2)}, u32[]{:S(2)}) collective-permute-start(bf16[384,768]{1,0:T(8,128)(2,1)} %get-tuple-element.214.refs_0_), channel_id=1, source_target_pairs={{0,16},{16,0},{1,17},{17,1},{2,18},{18,2},{3,19},{19,3},{4,20},{20... | collective-permute-start | bytes 1769480 | tf_op jit(solution)/shard_map/ppermute | solution.py:46
  116.8 19.0 %collective-permute-start.25 = (bf16[256,768]{1,0:T(8,128)(2,1)S(1)}, bf16[256,768]{1,0:T(8,128)(2,1)S(1)}, u32[]{:S(2)}, u32[]{:S(2)}) collective-permute-start(bf16[256,768]{1,0:T(8,128)(2,1)S(1)} %collective-permute-done.20.refs_4_), channel_id=1, source_target_pairs={{8,12},{4,0},{9,13},{5,1},{10,14},{6,2},{11,15},{7,3},{24,28},{20,... | collective-permute-start | bytes 1179656 | tf_op jit(solution)/shard_map/ppermute | solution.py:1168
  118.3 20.3 %collective-permute-start.29 = (bf16[256,768]{1,0:T(8,128)(2,1)S(1)}, bf16[256,768]{1,0:T(8,128)(2,1)}, u32[]{:S(2)}, u32[]{:S(2)}) collective-permute-start(bf16[256,768]{1,0:T(8,128)(2,1)S(1)} %copy-done.35), channel_id=1, source_target_pairs={{0,1},{1,0},{2,3},{3,2},{4,5},{5,4},{6,7},{7,6},{8,9},{9,8},{10,11... | collective-permute-start | bytes 1179656 | tf_op jit(solution)/shard_map/ppermute | solution.py:46
  135.9 4.2 collective-permute-start.28
  136.0 44.6 %collective-permute-start.30 = (bf16[432,512]{1,0:T(8,128)(2,1)S(1)}, bf16[432,512]{1,0:T(8,128)(2,1)S(1)}, u32[]{:S(2)}, u32[]{:S(2)}) collective-permute-start(bf16[432,512]{1,0:T(8,128)(2,1)S(1)} %copy-done.63), channel_id=1, source_target_pairs={{0,2},{1,3},{2,0},{3,1},{4,6},{5,7},{6,4},{7,5},{8,10},{9,11},{10,... | collective-permute-start | bytes 1327112 | tf_op jit(solution)/shard_map/ppermute | solution.py:46
  136.6 25.1 %collective-permute-start.34 = (bf16[384,768]{1,0:T(8,128)(2,1)}, bf16[384,768]{1,0:T(8,128)(2,1)S(1)}, u32[]{:S(2)}, u32[]{:S(2)}) collective-permute-start(bf16[384,768]{1,0:T(8,128)(2,1)} %get-tuple-element.214.refs_0_), channel_id=1, source_target_pairs={{0,2},{1,3},{2,0},{3,1},{4,6},{5,7},{6,4},{7,5},{8,10},{9,11},{10,... | collective-permute-start | bytes 1769480 | tf_op jit(solution)/shard_map/ppermute | solution.py:46
  138.1 36.2 %collective-permute-start.35 = (bf16[384,768]{1,0:T(8,128)(2,1)S(1)}, bf16[384,768]{1,0:T(8,128)(2,1)S(1)}, u32[]{:S(2)}, u32[]{:S(2)}) collective-permute-start(bf16[384,768]{1,0:T(8,128)(2,1)S(1)} %collective-permute-done.23.refs_2_), channel_id=1, source_target_pairs={{0,2},{1,3},{2,0},{3,1},{4,6},{5,7},{6,4},{7,5},{8,10},{9,11},{10,... | collective-permute-start | bytes 1769480 | tf_op jit(solution)/shard_map/ppermute | solution.py:46
  138.6 35.7 %collective-permute-start.32 = (bf16[384,1024]{1,0:T(8,128)(2,1)}, bf16[384,1024]{1,0:T(8,128)(2,1)S(1)}, u32[]{:S(2)}, u32[]{:S(2)}) collective-permute-start(bf16[384,1024]{1,0:T(8,128)(2,1)} %get-tuple-element.212.refs_0_), channel_id=1, source_target_pairs={{0,16},{16,0},{1,17},{17,1},{2,18},{18,2},{3,19},{19,3},{4,20},{20... | collective-permute-start | bytes 2359304 | tf_op jit(solution)/shard_map/ppermute | solution.py:46
  140.1 34.6 %collective-permute-start.33 = (bf16[384,1024]{1,0:T(8,128)(2,1)S(1)}, bf16[384,1024]{1,0:T(8,128)(2,1)S(1)}, u32[]{:S(2)}, u32[]{:S(2)}) collective-permute-start(bf16[384,1024]{1,0:T(8,128)(2,1)S(1)} %collective-permute-done.22.refs_1_), channel_id=1, source_target_pairs={{0,16},{16,0},{1,17},{17,1},{2,18},{18,2},{3,19},{19,3},{4,20},{20... | collective-permute-start | bytes 2359304 | tf_op jit(solution)/shard_map/ppermute | solution.py:46
  161.7 21.7 %collective-permute-start.31 = (bf16[432,512]{1,0:T(8,128)(2,1)}, bf16[432,512]{1,0:T(8,128)(2,1)S(1)}, u32[]{:S(2)}, u32[]{:S(2)}) collective-permute-start(bf16[432,512]{1,0:T(8,128)(2,1)} %get-tuple-element.210), channel_id=1, source_target_pairs={{0,2},{1,3},{2,0},{3,1},{4,6},{5,7},{6,4},{7,5},{8,10},{9,11},{10,... | collective-permute-start | bytes 1327112 | tf_op jit(solution)/shard_map/ppermute | solution.py:46
  196.0 4.7 collective-permute-start.37
  262.8 13.2 %collective-permute-start.42 = (bf16[432,512]{1,0:T(8,128)(2,1)}, bf16[432,512]{1,0:T(8,128)(2,1)S(1)}, u32[]{:S(2)}, u32[]{:S(2)}) collective-permute-start(bf16[432,512]{1,0:T(8,128)(2,1)} %get-tuple-element.241.g_own), channel_id=1, source_target_pairs={{0,2},{1,3},{2,0},{3,1},{4,6},{5,7},{6,4},{7,5},{8,10},{9,11},{10,... | collective-permute-start | bytes 1327112 | tf_op jit(solution)/shard_map/ppermute | solution.py:46
  263.4 62.7 %collective-permute-start.49 = (bf16[384,3072]{1,0:T(8,128)(2,1)S(1)}, bf16[384,3072]{1,0:T(8,128)(2,1)S(1)}, u32[]{:S(2)}, u32[]{:S(2)}) collective-permute-start(bf16[384,3072]{1,0:T(8,128)(2,1)S(1)} %copy-done.60), channel_id=1, source_target_pairs={{0,16},{16,0},{1,17},{17,1},{2,18},{18,2},{3,19},{19,3},{4,20},{20... | collective-permute-start | bytes 7077896 | tf_op jit(solution)/shard_map/ppermute | solution.py:46
  264.9 6.6 %collective-permute-start.43 = (f32[6,768]{1,0:T(8,128)S(1)}, f32[6,768]{1,0:T(8,128)S(1)}, u32[]{:S(2)}, u32[]{:S(2)}) collective-permute-start(f32[6,768]{1,0:T(8,128)S(1)} %pad_maximum_fusion.1), channel_id=1, source_target_pairs={{0,1},{1,0},{2,3},{3,2},{4,5},{5,4},{6,7},{7,6},{8,9},{9,8},{10,11... | collective-permute-start | bytes 55304 | tf_op jit(solution)/shard_map/ppermute | solution.py:46
  265.0 58.0 %collective-permute-start.44 = (bf16[432,512]{1,0:T(8,128)(2,1)}, bf16[432,512]{1,0:T(8,128)(2,1)S(1)}, u32[]{:S(2)}, u32[]{:S(2)}) collective-permute-start(bf16[432,512]{1,0:T(8,128)(2,1)} %get-tuple-element.248.g_own), channel_id=1, source_target_pairs={{0,2},{1,3},{2,0},{3,1},{4,6},{5,7},{6,4},{7,5},{8,10},{9,11},{10,... | collective-permute-start | bytes 1327112 | tf_op jit(solution)/shard_map/ppermute | solution.py:46
  271.0 52.0 %collective-permute-start.45 = (bf16[384,384]{1,0:T(8,128)(2,1)}, bf16[384,384]{1,0:T(8,128)(2,1)S(1)}, u32[]{:S(2)}, u32[]{:S(2)}) collective-permute-start(bf16[384,384]{1,0:T(8,128)(2,1)} %get-tuple-element.253), channel_id=1, source_target_pairs={{0,16},{16,0},{1,17},{17,1},{2,18},{18,2},{3,19},{19,3},{4,20},{20... | collective-permute-start | bytes 884744 | tf_op jit(solution)/shard_map/ppermute | solution.py:46
  276.1 46.9 %collective-permute-start.46 = (f32[1,6144]{1,0:T(1,128)S(1)}, f32[1,6144]{1,0:T(1,128)S(1)}, u32[]{:S(2)}, u32[]{:S(2)}) collective-permute-start(f32[1,6144]{1,0:T(1,128)S(1)} %constant_dynamic-update-slice_fusion.6), channel_id=1, source_target_pairs={{0,4},{4,0},{8,12},{12,8},{1,5},{5,1},{9,13},{13,9},{2,6},{6,2},{1... | collective-permute-start | bytes 73736 | tf_op jit(solution)/shard_map/ppermute | solution.py:46
  323.0 8.7 %collective-permute-start.50 = (bf16[1024,768]{1,0:T(8,128)(2,1)}, bf16[1024,768]{1,0:T(8,128)(2,1)S(1)}, u32[]{:S(2)}, u32[]{:S(2)}) collective-permute-start(bf16[1024,768]{1,0:T(8,128)(2,1)} %get-tuple-element.265), channel_id=1, source_target_pairs={{0,1},{1,0},{2,3},{3,2},{4,5},{5,4},{6,7},{7,6},{8,9},{9,8},{10,11... | collective-permute-start | bytes 4718600 | tf_op jit(solution)/shard_map/ppermute | solution.py:46
  323.1 14.8 %collective-permute-start.48 = (f32[1,6144]{1,0:T(1,128)S(1)}, f32[1,6144]{1,0:T(1,128)S(1)}, u32[]{:S(2)}, u32[]{:S(2)}) collective-permute-start(f32[1,6144]{1,0:T(1,128)S(1)} %add.120), channel_id=1, source_target_pairs={{0,8},{4,12},{8,0},{12,4},{1,9},{5,13},{9,1},{13,5},{2,10},{6,14},... | collective-permute-start | bytes 73736 | tf_op jit(solution)/shard_map/ppermute | solution.py:46
  324.5 13.9 %collective-permute-start.47 = (bf16[384,512]{1,0:T(8,128)(2,1)}, bf16[384,512]{1,0:T(8,128)(2,1)S(1)}, u32[]{:S(2)}, u32[]{:S(2)}) collective-permute-start(bf16[384,512]{1,0:T(8,128)(2,1)} %get-tuple-element.257), channel_id=1, source_target_pairs={{0,2},{1,3},{2,0},{3,1},{4,6},{5,7},{6,4},{7,5},{8,10},{9,11},{10,... | collective-permute-start | bytes 1179656 | tf_op jit(solution)/shard_map/ppermute | solution.py:46
  331.2 30.0 %collective-permute-start.51 = (bf16[384,1536]{1,0:T(8,128)(2,1)}, bf16[384,1536]{1,0:T(8,128)(2,1)S(1)}, u32[]{:S(2)}, u32[]{:S(2)}) collective-permute-start(bf16[384,1536]{1,0:T(8,128)(2,1)} %get-tuple-element.263), channel_id=1, source_target_pairs={{0,2},{1,3},{2,0},{3,1},{4,6},{5,7},{6,4},{7,5},{8,10},{9,11},{10,... | collective-permute-start | bytes 3538952 | tf_op jit(solution)/shard_map/ppermute | solution.py:46
  333.9 27.3 %collective-permute-start.54 = (bf16[256,768]{1,0:T(8,128)(2,1)S(1)}, bf16[256,768]{1,0:T(8,128)(2,1)S(1)}, u32[]{:S(2)}, u32[]{:S(2)}) collective-permute-start(bf16[256,768]{1,0:T(8,128)(2,1)S(1)} %get-tuple-element.362), channel_id=1, source_target_pairs={{0,12},{4,8},{8,4},{12,0},{1,13},{5,9},{9,5},{13,1},{2,14},{6,10},... | collective-permute-start | bytes 1179656 | tf_op jit(solution)/shard_map/ppermute | solution.py:46
  336.0 35.7 %collective-permute-start.53 = (bf16[256,768]{1,0:T(8,128)(2,1)S(1)}, bf16[256,768]{1,0:T(8,128)(2,1)S(1)}, u32[]{:S(2)}, u32[]{:S(2)}) collective-permute-start(bf16[256,768]{1,0:T(8,128)(2,1)S(1)} %get-tuple-element.363), channel_id=1, source_target_pairs={{0,8},{4,12},{8,0},{12,4},{1,9},{5,13},{9,1},{13,5},{2,10},{6,14},... | collective-permute-start | bytes 1179656 | tf_op jit(solution)/shard_map/ppermute | solution.py:46
  337.9 33.8 %collective-permute-start.52 = (bf16[256,768]{1,0:T(8,128)(2,1)S(1)}, bf16[256,768]{1,0:T(8,128)(2,1)S(1)}, u32[]{:S(2)}, u32[]{:S(2)}) collective-permute-start(bf16[256,768]{1,0:T(8,128)(2,1)S(1)} %get-tuple-element.364), channel_id=1, source_target_pairs={{0,4},{4,0},{8,12},{12,8},{1,5},{5,1},{9,13},{13,9},{2,6},{6,2},{1... | collective-permute-start | bytes 1179656 | tf_op jit(solution)/shard_map/ppermute | solution.py:46
  371.7 25.6 %collective-permute-start.56 = (bf16[1024,768]{1,0:T(8,128)(2,1)}, bf16[1024,768]{1,0:T(8,128)(2,1)S(1)}, u32[]{:S(2)}, u32[]{:S(2)}) collective-permute-start(bf16[1024,768]{1,0:T(8,128)(2,1)} %get-tuple-element.279), channel_id=1, source_target_pairs={{0,1},{1,0},{2,3},{3,2},{4,5},{5,4},{6,7},{7,6},{8,9},{9,8},{10,11... | collective-permute-start | bytes 4718600 | tf_op jit(solution)/shard_map/ppermute | solution.py:46
  374.6 62.2 %all-to-all-start = ((bf16[4,96,1536]{2,1,0:T(8,128)(2,1)}), bf16[4,96,1536]{2,1,0:T(8,128)(2,1)S(1)}, u32[]{:S(2)}, u32[]{:S(2)}) async-start(bf16[4,96,1536]{2,1,0:T(8,128)(2,1)} %bitcast.48), calls=%async_computation | async-start | bytes 2359296 | tf_op jit(solution)/shard_map/all_to_all | solution.py:1362
  378.1 33.3 %collective-permute-start.55 = (bf16[384,512]{1,0:T(8,128)(2,1)}, bf16[384,512]{1,0:T(8,128)(2,1)S(1)}, u32[]{:S(2)}, u32[]{:S(2)}) collective-permute-start(bf16[384,512]{1,0:T(8,128)(2,1)} %get-tuple-element.275), channel_id=1, source_target_pairs={{0,2},{1,3},{2,0},{3,1},{4,6},{5,7},{6,4},{7,5},{8,10},{9,11},{10,... | collective-permute-start | bytes 1179656 | tf_op jit(solution)/shard_map/ppermute | solution.py:46
  379.8 47.5 %collective-permute-start.59 = (bf16[384,768]{1,0:T(8,128)(2,1)}, bf16[384,768]{1,0:T(8,128)(2,1)S(1)}, u32[]{:S(2)}, u32[]{:S(2)}) collective-permute-start(bf16[384,768]{1,0:T(8,128)(2,1)} %get-tuple-element.287), channel_id=1, source_target_pairs={{0,16},{16,0},{1,17},{17,1},{2,18},{18,2},{3,19},{19,3},{4,20},{20... | collective-permute-start | bytes 1769480 | tf_op jit(solution)/shard_map/ppermute | solution.py:46
  403.4 23.9 %collective-permute-start.62 = (bf16[256,768]{1,0:T(8,128)(2,1)}, bf16[256,768]{1,0:T(8,128)(2,1)}, u32[]{:S(2)}, u32[]{:S(2)}) collective-permute-start(bf16[256,768]{1,0:T(8,128)(2,1)} %get-tuple-element.360), channel_id=1, source_target_pairs={{4,8},{8,4},{5,9},{9,5},{6,10},{10,6},{7,11},{11,7},{20,24},{24,20... | collective-permute-start | bytes 1179656 | tf_op jit(solution)/shard_map/ppermute | solution.py:1378
  404.8 22.5 %collective-permute-start.61 = (bf16[256,768]{1,0:T(8,128)(2,1)}, bf16[256,768]{1,0:T(8,128)(2,1)}, u32[]{:S(2)}, u32[]{:S(2)}) collective-permute-start(bf16[256,768]{1,0:T(8,128)(2,1)} %get-tuple-element.360), channel_id=1, source_target_pairs={{12,8},{0,4},{13,9},{1,5},{14,10},{2,6},{15,11},{3,7},{28,24},{16,... | collective-permute-start | bytes 1179656 | tf_op jit(solution)/shard_map/ppermute | solution.py:1377
  419.3 8.0 %collective-permute-start.58 = (bf16[384,384]{1,0:T(8,128)(2,1)}, bf16[384,384]{1,0:T(8,128)(2,1)S(1)}, u32[]{:S(2)}, u32[]{:S(2)}) collective-permute-start(bf16[384,384]{1,0:T(8,128)(2,1)} %get-tuple-element.286), channel_id=1, source_target_pairs={{0,16},{16,0},{1,17},{17,1},{2,18},{18,2},{3,19},{19,3},{4,20},{20... | collective-permute-start | bytes 884744 | tf_op jit(solution)/shard_map/ppermute | solution.py:46
  419.4 7.9 %collective-permute-start.60 = (f32[1,6912]{1,0:T(1,128)S(1)}, f32[1,6912]{1,0:T(1,128)S(1)}, u32[]{:S(2)}, u32[]{:S(2)}) collective-permute-start(f32[1,6912]{1,0:T(1,128)S(1)} %constant_dynamic-update-slice_fusion.8), channel_id=1, source_target_pairs={{0,16},{16,0},{1,17},{17,1},{2,18},{18,2},{3,19},{19,3},{4,20},{20... | collective-permute-start | bytes 82952 | tf_op jit(solution)/shard_map/ppermute | solution.py:46
  427.2 9.4 %collective-permute-start.57 = (bf16[512,768]{1,0:T(8,128)(2,1)}, bf16[512,768]{1,0:T(8,128)(2,1)S(1)}, u32[]{:S(2)}, u32[]{:S(2)}) collective-permute-start(bf16[512,768]{1,0:T(8,128)(2,1)} %get-tuple-element.282), channel_id=1, source_target_pairs={{0,1},{1,0},{2,3},{3,2},{4,5},{5,4},{6,7},{7,6},{8,9},{9,8},{10,11... | collective-permute-start | bytes 2359304 | tf_op jit(solution)/shard_map/ppermute | solution.py:46
  432.6 21.4 %collective-permute-start.63 = (bf16[384,768]{1,0:T(8,128)(2,1)}, bf16[384,768]{1,0:T(8,128)(2,1)S(1)}, u32[]{:S(2)}, u32[]{:S(2)}) collective-permute-start(bf16[384,768]{1,0:T(8,128)(2,1)} %get-tuple-element.301), channel_id=1, source_target_pairs={{0,2},{1,3},{2,0},{3,1},{4,6},{5,7},{6,4},{7,5},{8,10},{9,11},{10,... | collective-permute-start | bytes 1769480 | tf_op jit(solution)/shard_map/ppermute | solution.py:46
  433.1 18.9 %collective-permute-start.66 = (bf16[256,768]{1,0:T(8,128)(2,1)}, bf16[256,768]{1,0:T(8,128)(2,1)}, u32[]{:S(2)}, u32[]{:S(2)}) collective-permute-start(bf16[256,768]{1,0:T(8,128)(2,1)} %get-tuple-element.361), channel_id=1, source_target_pairs={{0,4},{4,0},{8,12},{12,8},{1,5},{5,1},{9,13},{13,9},{2,6},{6,2},{1... | collective-permute-start | bytes 1179656 | tf_op jit(solution)/shard_map/ppermute | solution.py:46
  433.1 20.9 %collective-permute-start.65 = (bf16[256,768]{1,0:T(8,128)(2,1)}, bf16[256,768]{1,0:T(8,128)(2,1)}, u32[]{:S(2)}, u32[]{:S(2)}) collective-permute-start(bf16[256,768]{1,0:T(8,128)(2,1)} %add_convert_fusion), channel_id=1, source_target_pairs={{0,8},{4,12},{8,0},{12,4},{1,9},{5,13},{9,1},{13,5},{2,10},{6,14},... | collective-permute-start | bytes 1179656 | tf_op jit(solution)/shard_map/ppermute | solution.py:46
  435.1 16.8 %collective-permute-start.64 = (f32[1,6912]{1,0:T(1,128)S(1)}, f32[1,6912]{1,0:T(1,128)S(1)}, u32[]{:S(2)}, u32[]{:S(2)}) collective-permute-start(f32[1,6912]{1,0:T(1,128)S(1)} %add.132), channel_id=1, source_target_pairs={{0,2},{1,3},{2,0},{3,1},{4,6},{5,7},{6,4},{7,5},{8,10},{9,11},{10,... | collective-permute-start | bytes 82952 | tf_op jit(solution)/shard_map/ppermute | solution.py:46
  457.0 8.9 %collective-permute-start.67 = (bf16[112,768]{1,0:T(8,128)(2,1)}, bf16[112,768]{1,0:T(8,128)(2,1)S(1)}, u32[]{:S(2)}, u32[]{:S(2)}) collective-permute-start(bf16[112,768]{1,0:T(8,128)(2,1)} %get-tuple-element.309), channel_id=1, source_target_pairs={{0,4},{4,0},{8,12},{12,8},{1,5},{5,1},{9,13},{13,9},{2,6},{6,2},{1... | collective-permute-start | bytes 516104 | tf_op jit(solution)/shard_map/ppermute | solution.py:46
  457.0 15.8 %collective-permute-start.68 = (bf16[112,768]{1,0:T(8,128)(2,1)}, bf16[112,768]{1,0:T(8,128)(2,1)S(1)}, u32[]{:S(2)}, u32[]{:S(2)}) collective-permute-start(bf16[112,768]{1,0:T(8,128)(2,1)} %get-tuple-element.310), channel_id=1, source_target_pairs={{0,8},{4,12},{8,0},{12,4},{1,9},{5,13},{9,1},{13,5},{2,10},{6,14},... | collective-permute-start | bytes 516104 | tf_op jit(solution)/shard_map/ppermute | solution.py:46
  459.1 13.7 %collective-permute-start.69 = (bf16[112,768]{1,0:T(8,128)(2,1)}, bf16[112,768]{1,0:T(8,128)(2,1)S(1)}, u32[]{:S(2)}, u32[]{:S(2)}) collective-permute-start(bf16[112,768]{1,0:T(8,128)(2,1)} %get-tuple-element.311), channel_id=1, source_target_pairs={{0,12},{4,8},{8,4},{12,0},{1,13},{5,9},{9,5},{13,1},{2,14},{6,10},... | collective-permute-start | bytes 516104 | tf_op jit(solution)/shard_map/ppermute | solution.py:46
  (83 other events, 903.6 us)
